TPU v7x, 32 devices: a whole 2x2x4 slice. The times are simulated.
32 devices in a mesh: blk: 8 (over z, x), grp: 4 (over y, core).
Axes of the slice: x: 2, y: 2, z: 4, core: 2. Of those that a mesh axis runs over, the one named last changes fastest.
Arguments:
- tokens: bfloat16 [512, 8192], P(('blk', 'grp')), may hold values from -6 to 6
- cotangent: bfloat16 [512, 8192], P(('blk', 'grp')), may hold values from -6 to 6
- gate_weight: bfloat16 [8192, 4096], P(None, 'blk'), may hold values from -0.0625 to 0.0625
- up_weight: bfloat16 [8192, 4096], P(None, 'blk'), may hold values from -0.0625 to 0.0625
- down_weight: bfloat16 [4096, 8192], P('blk'), may hold values from -0.09375 to 0.09375
- a_gate: bfloat16 [256, 16, 8192], P('blk'), may hold values from -0.0625 to 0.0625
- a_up: bfloat16 [256, 16, 8192], P('blk'), may hold values from -0.0625 to 0.0625
- down_output_factors: bfloat16 [256, 16, 8192], P('blk'), may hold values from -0.375 to 0.375
- b_gate: bfloat16 [256, 16, 4096], P(None, None, 'blk'), may hold values from -0.375 to 0.375
- b_up: bfloat16 [256, 16, 4096], P(None, None, 'blk'), may hold values from -0.375 to 0.375
- a_down: bfloat16 [256, 16, 4096], P(None, None, 'blk'), may hold values from -0.09375 to 0.09375
- tenant_of_row: int32 [512], replicated, may hold values from 0 to 255, as said below
- adapter_slot: int32 [256], replicated, may hold values from 0 to 255, as said below
Outputs:
- mixed: bfloat16 [512, 8192], P(('blk', 'grp'))
- input_grad: bfloat16 [512, 8192], P(('blk', 'grp'))
- grad_a_gate: float32 [256, 16, 8192], P(('blk', 'grp'))
- grad_a_up: float32 [256, 16, 8192], P(('blk', 'grp'))
- grad_b_down: float32 [256, 16, 8192], P(('blk', 'grp'))
- grad_b_gate: float32 [256, 16, 4096], P('grp', None, 'blk')
- grad_b_up: float32 [256, 16, 4096], P('grp', None, 'blk')
- grad_a_down: float32 [256, 16, 4096], P('grp', None, 'blk')
Inputs may be any that keep to these rules, and one draw needn't show every extreme that they name: `tenant_of_row`: among the rows held by the devices of one index of grp, for each index b of blk at most 32 rows have tenants whose adapter slot s has s // 32 == b, and for some b exactly 32 do. A permutation: tenant t's factors in a_gate, a_up and down_output_factors, and its gradients of them, stand at index adapter_slot[t].
All inputs are finite; a program needn't handle non-finite values.
Results may differ from a plain program's by a relative error of at most 0.02.
Values may be sent and summed in bfloat16 or wider, within the bound.
A program may use at most 192 MiB of HBM per device.

v0:
```python
import functools

import jax
import jax.numpy as jnp
from jax import lax
from jax.experimental import pallas as pl
from jax.experimental.pallas import tpu as pltpu
from jax.sharding import PartitionSpec as P

MESH = pl.DeviceIdType.MESH
bf16 = jnp.bfloat16
f32 = jnp.float32


def remote(src, dst, send, recv, to):
    return pltpu.make_async_remote_copy(
        src_ref=src,
        dst_ref=dst,
        send_sem=send,
        recv_sem=recv,
        device_id={"blk": to},
        device_id_type=MESH,
    )


def place(blocks):
    me = lax.axis_index("blk")
    line = blocks // 2
    row = me // 2
    col = me - 2 * row
    partner = me + 1 - 2 * col
    return me, line, row, col, partner


def greet(me, line, row, partner):
    barrier = pltpu.get_barrier_semaphore()
    pl.semaphore_signal(barrier, inc=1, device_id={"blk": partner}, device_id_type=MESH)

    @pl.when(row < line - 1)
    def _():
        pl.semaphore_signal(barrier, inc=1, device_id={"blk": me + 2}, device_id_type=MESH)

    @pl.when(row > 0)
    def _():
        pl.semaphore_signal(barrier, inc=1, device_id={"blk": me - 2}, device_id_type=MESH)

    peers = 1 + (row < line - 1).astype(jnp.int32) + (row > 0).astype(jnp.int32)
    pl.semaphore_wait(barrier, peers)


def gather_kernel(
    blocks, x_ref, d_ref, xo_ref, do_ref, own_sem, up_s, up_r, dn_s, dn_r, ac_s, ac_r, ex_s, ex_r
):
    me, line, row, col, partner = place(blocks)
    outs = (xo_ref, do_ref)
    ins = (x_ref, d_ref)
    above, below = me + 2, me - 2

    def up_copy(c, src, block, s):
        return remote(src, outs[c].at[block], up_s.at[c, s], up_r.at[c, s], above)

    def dn_copy(c, src, block, s):
        return remote(src, outs[c].at[block], dn_s.at[c, s], dn_r.at[c, s], below)

    def ac_copy(c, src, at):
        return remote(
            src, outs[c].at[2 * at + col], ac_s.at[c, at], ac_r.at[c, at], partner
        )

    def ac_arrival(c, at):
        ref = outs[c].at[2 * at + 1 - col]
        return remote(ref, ref, ac_s.at[c, at], ac_r.at[c, at], partner)

    def ex_copy(direction, to):
        ref = do_ref.at[partner]
        return remote(ref, ref, ex_s.at[direction], ex_r.at[direction], to)

    def ex_arrival(direction, block, to):
        ref = do_ref.at[block]
        return remote(ref, ref, ex_s.at[direction], ex_r.at[direction], to)

    greet(me, line, row, partner)
    own = []
    for c in range(2):
        ac_copy(c, ins[c], row).start()

        @pl.when(row < line - 1)
        def _():
            up_copy(c, ins[c], me, 0).start()

        @pl.when(row > 0)
        def _():
            dn_copy(c, ins[c], me, 0).start()

    for c in range(2):
        copy = pltpu.make_async_copy(ins[c], outs[c].at[me], own_sem.at[c])
        copy.start()
        own.append(copy)
    for s in range(1, line):
        for c in range(2):

            @pl.when(row >= s)
            def _():
                block = me - 2 * s
                ref = outs[c].at[block]
                up_copy(c, ref, block, s - 1).wait_recv()
                if s < line - 1:

                    @pl.when(row < line - 1)
                    def _():
                        up_copy(c, ref, block, s).start()

                if c == 0 or s > 1:
                    ac_copy(c, ref, row - s).start()

            @pl.when(row + s < line)
            def _():
                block = me + 2 * s
                ref = outs[c].at[block]
                dn_copy(c, ref, block, s - 1).wait_recv()
                if s < line - 1:

                    @pl.when(row > 0)
                    def _():
                        dn_copy(c, ref, block, s).start()

                if c == 0 or s > 1:
                    ac_copy(c, ref, row + s).start()

        if s == 1:
            ac_arrival(1, row).wait_recv()

            @pl.when(row < line - 1)
            def _():
                ex_copy(0, above).start()

            @pl.when(row > 0)
            def _():
                ex_copy(1, below).start()

    ac_arrival(0, row).wait_recv()
    ac_copy(0, x_ref, row).wait_send()
    ac_copy(1, d_ref, row).wait_send()
    for s in range(1, line):
        for c in range(2):
            for ok, at in ((row >= s, row - s), (row + s < line, row + s)):

                @pl.when(ok)
                def _():
                    if c == 0 or s > 1:
                        ac_arrival(c, at).wait_recv()
                        ac_copy(c, outs[c].at[2 * at + col], at).wait_send()

    @pl.when(row > 0)
    def _():
        ex_arrival(0, partner - 2, above).wait_recv()
        ex_copy(1, below).wait_send()

    @pl.when(row < line - 1)
    def _():
        ex_arrival(1, partner + 2, below).wait_recv()
        ex_copy(0, above).wait_send()

    for s in range(line - 1):
        for c in range(2):

            @pl.when((row >= s) & (row < line - 1))
            def _():
                src = ins[c] if s == 0 else outs[c].at[me - 2 * s]
                up_copy(c, src, me - 2 * s, s).wait_send()

            @pl.when((row + s < line) & (row > 0))
            def _():
                src = ins[c] if s == 0 else outs[c].at[me + 2 * s]
                dn_copy(c, src, me + 2 * s, s).wait_send()

    for copy in own:
        copy.wait()


def gather_rows(blocks, x, dy):
    line = blocks // 2
    shape = jax.ShapeDtypeStruct((blocks,) + x.shape, x.dtype)
    dma = pltpu.SemaphoreType.DMA
    got = pl.pallas_call(
        functools.partial(gather_kernel, blocks),
        out_shape=(shape, shape),
        in_specs=[pl.BlockSpec(memory_space=pltpu.VMEM)] * 2,
        out_specs=(pl.BlockSpec(memory_space=pl.ANY),) * 2,
        scratch_shapes=[dma((2,))] + [dma((2, line))] * 6 + [dma((2,))] * 2,
        compiler_params=pltpu.CompilerParams(
            collective_id=0, has_side_effects=True, vmem_limit_bytes=4 * 2**20
        ),
        name="gather_rows",
    )(x, dy)
    return [part.reshape((-1,) + x.shape[1:]) for part in got]


def scatter_kernel(
    blocks,
    m_ref,
    b_ref,
    mo_ref,
    bo_ref,
    pair_buf,
    line_buf,
    top_buf,
    ex_buf,
    cross_buf,
    ac_s,
    ac_r,
    up_s,
    up_r,
    dn_s,
    dn_r,
    ex_s,
    ex_r,
):
    me, line, row, col, partner = place(blocks)
    parts = (m_ref, b_ref)
    outs = (mo_ref, bo_ref)
    above, below = me + 2, me - 2
    width = m_ref.shape[-1]
    tile = width // 8

    def total(dst, srcs):
        def body(k, carry):
            at = pl.ds(pl.multiple_of(k * tile, tile), tile)
            acc = srcs[0][:, at].astype(f32)
            for src in srcs[1:]:
                acc = acc + src[:, at].astype(f32)
            dst[:, at] = acc.astype(dst.dtype)
            return carry

        lax.fori_loop(0, width // tile, body, 0)

    def ac_copy(c, src, at):
        return remote(src, pair_buf.at[c, at], ac_s.at[c, at], ac_r.at[c, at], partner)

    def up_copy(c, at):
        return remote(
            pair_buf.at[c, at], line_buf.at[c, at], up_s.at[c, at], up_r.at[c, at], above
        )

    def dn_copy(c, at, landing):
        return remote(pair_buf.at[c, at], landing, dn_s.at[c, at], dn_r.at[c, at], below)

    def ex_copy(direction, block, to):
        return remote(
            b_ref.at[block], ex_buf.at[direction], ex_s.at[direction], ex_r.at[direction], to
        )

    greet(me, line, row, partner)

    @pl.when(row < line - 1)
    def _():
        ex_copy(0, partner + 2, above).start()

    @pl.when(row > 0)
    def _():
        ex_copy(1, partner - 2, below).start()

    def spots(s):
        if s == 0:
            return ((None, row),)
        return ((row + s < line, row + s), (row >= s, row - s))

    def crossing(c, s):
        return c == 0 or s > 1

    def guard(ok, body):
        if ok is None:
            body()
        else:
            pl.when(ok)(body)

    for s in range(line - 1, -1, -1):
        for c in range(2):
            for ok, at in spots(s):
                if crossing(c, s):
                    guard(ok, lambda: ac_copy(c, parts[c].at[2 * at + 1 - col], at).start())

    @pl.when(row > 0)
    def _():
        ex_copy(0, partner, above).wait_recv()

    @pl.when(row < line - 1)
    def _():
        ex_copy(1, partner, below).wait_recv()

    @pl.when((row > 0) & (row < line - 1))
    def _():
        total(cross_buf, (b_ref.at[partner], ex_buf.at[0], ex_buf.at[1]))

    @pl.when(row == 0)
    def _():
        total(cross_buf, (b_ref.at[partner], ex_buf.at[1]))

    @pl.when((row > 0) & (row == line - 1))
    def _():
        total(cross_buf, (b_ref.at[partner], ex_buf.at[0]))

    ac_copy(1, cross_buf, row).start()

    for s in range(line - 1, 0, -1):
        for c in range(2):

            @pl.when(row + s < line)
            def _():
                at = row + s
                slot = pair_buf.at[c, at]
                mine = parts[c].at[2 * at + col]
                base = (mine,)
                if crossing(c, s):
                    ac_copy(c, mine, at).wait_recv()
                    base = (mine, slot)
                if s < line - 1:

                    @pl.when(row > 0)
                    def _():
                        up_copy(c, at).wait_recv()
                        total(slot, base + (line_buf.at[c, at],))

                @pl.when(row == 0)
                def _():
                    total(slot, base)

                up_copy(c, at).start()

            @pl.when(row >= s)
            def _():
                at = row - s
                slot = pair_buf.at[c, at]
                mine = parts[c].at[2 * at + col]
                base = (mine,)
                if crossing(c, s):
                    ac_copy(c, mine, at).wait_recv()
                    base = (mine, slot)
                if s < line - 1:

                    @pl.when(row < line - 1)
                    def _():
                        dn_copy(c, at, line_buf.at[c, at]).wait_recv()
                        total(slot, base + (line_buf.at[c, at],))

                @pl.when(row == line - 1)
                def _():
                    total(slot, base)

                if s == 1:
                    dn_copy(c, at, top_buf.at[c]).start()
                else:
                    dn_copy(c, at, line_buf.at[c, at]).start()

    for c in range(2):
        mine = parts[c].at[me]
        slot = pair_buf.at[c, row]
        from_below = line_buf.at[c, row]
        from_above = top_buf.at[c]
        ac_copy(c, mine, row).wait_recv()

        @pl.when(row > 0)
        def _():
            up_copy(c, row).wait_recv()

        @pl.when(row < line - 1)
        def _():
            dn_copy(c, row, from_above).wait_recv()

        @pl.when((row > 0) & (row < line - 1))
        def _():
            total(outs[c], (mine, slot, from_below, from_above))

        @pl.when(row == 0)
        def _():
            total(outs[c], (mine, slot, from_above))

        @pl.when((row > 0) & (row == line - 1))
        def _():
            total(outs[c], (mine, slot, from_below))

    ac_copy(0, m_ref.at[partner], row).wait_send()
    ac_copy(1, cross_buf, row).wait_send()
    for s in range(1, line):
        for c in range(2):
            for ok, at in spots(s):
                if crossing(c, s):
                    guard(ok, lambda: ac_copy(c, parts[c].at[2 * at + 1 - col], at).wait_send())

            @pl.when(row + s < line)
            def _():
                up_copy(c, row + s).wait_send()

            @pl.when(row >= s)
            def _():
                dn_copy(c, row - s, line_buf.at[c, row - s]).wait_send()

    @pl.when(row < line - 1)
    def _():
        ex_copy(0, partner + 2, above).wait_send()

    @pl.when(row > 0)
    def _():
        ex_copy(1, partner - 2, below).wait_send()


def scatter_rows(blocks, mixed_terms, back_terms):
    line = blocks // 2
    rows = mixed_terms.shape[0] // blocks
    width = mixed_terms.shape[1]
    dma = pltpu.SemaphoreType.DMA
    block = jax.ShapeDtypeStruct((rows, width), bf16)
    block_bytes = 2 * rows * width
    return pl.pallas_call(
        functools.partial(scatter_kernel, blocks),
        out_shape=(block, block),
        in_specs=[pl.BlockSpec(memory_space=pltpu.VMEM)] * 2,
        out_specs=(pl.BlockSpec(memory_space=pltpu.VMEM),) * 2,
        scratch_shapes=[
            pltpu.VMEM((2, line, rows, width), bf16),
            pltpu.VMEM((2, line, rows, width), bf16),
            pltpu.VMEM((2, rows, width), bf16),
            pltpu.VMEM((2, rows, width), bf16),
            pltpu.VMEM((rows, width), bf16),
        ]
        + [dma((2, line))] * 6
        + [dma((2,))] * 2,
        compiler_params=pltpu.CompilerParams(
            collective_id=3,
            has_side_effects=True,
            vmem_limit_bytes=block_bytes * (2 * blocks + 4 * line + 12) + 2 * 2**20,
        ),
        name="scatter_rows",
    )(
        mixed_terms.reshape(blocks, rows, width),
        back_terms.reshape(blocks, rows, width),
    )


def sum_kernel(blocks, c_ref, o_ref, land, send_sem, recv_sem):
    me = lax.axis_index("blk")
    barrier = pltpu.get_barrier_semaphore()
    for k in range(1, blocks):
        pl.semaphore_signal(
            barrier, inc=1, device_id={"blk": lax.rem(me + k, blocks)}, device_id_type=MESH
        )
    pl.semaphore_wait(barrier, blocks - 1)
    copies = []
    for k in range(1, blocks):
        copy = remote(
            c_ref, land.at[k], send_sem.at[k], recv_sem.at[k], lax.rem(me + k, blocks)
        )
        copy.start()
        copies.append(copy)
    acc = c_ref[...].astype(f32)
    for k in range(1, blocks):
        copies[k - 1].wait_recv()
        acc = acc + land[k].astype(f32)
    o_ref[...] = acc.astype(o_ref.dtype)
    for copy in copies:
        copy.wait_send()


def sum_over_blk(blocks, coeffs, collective_id):
    dma = pltpu.SemaphoreType.DMA
    return pl.pallas_call(
        functools.partial(sum_kernel, blocks),
        out_shape=jax.ShapeDtypeStruct(coeffs.shape, coeffs.dtype),
        in_specs=[pl.BlockSpec(memory_space=pltpu.VMEM)],
        out_specs=pl.BlockSpec(memory_space=pltpu.VMEM),
        scratch_shapes=[
            pltpu.VMEM((blocks,) + coeffs.shape, coeffs.dtype),
            dma((blocks,)),
            dma((blocks,)),
        ],
        compiler_params=pltpu.CompilerParams(
            collective_id=collective_id, has_side_effects=True, vmem_limit_bytes=8 * 2**20
        ),
        name="sum_over_blk",
    )(coeffs)


adapter_scale = 2.0


def silu_pair(gate_in):
    sigmoid_val = jax.nn.sigmoid(gate_in)
    return (gate_in * sigmoid_val, sigmoid_val * (1.0 + gate_in * (1.0 - sigmoid_val)))


def dot(a, b, dims=((1,), (0,))):
    return lax.dot_general(a, b, (dims, ((), ())), preferred_element_type=f32)


def ranks_pattern(rank, entries):
    column = lax.broadcasted_iota(jnp.int32, (rank, entries * rank), 1)
    row = lax.broadcasted_iota(jnp.int32, (rank, entries * rank), 0)
    return (column % rank == row).astype(bf16)


def local(
    tokens,
    cotangent,
    gate_weight,
    up_weight,
    down_weight,
    a_gate,
    a_up,
    down_output_factors,
    b_gate,
    b_up,
    a_down,
    tenant_of_row,
    adapter_slot,
):
    own_rows, width = tokens.shape
    blocks = lax.axis_size("blk")
    grp_count = lax.axis_size("grp")
    blk_index = lax.axis_index("blk")
    grp_index = lax.axis_index("grp")
    per_owner, rank = a_gate.shape[:2]
    tenant_count, _, units = b_gate.shape
    capacity = 2 * own_rows
    group_rows = own_rows * blocks
    x, dy = gather_rows(blocks, tokens, cotangent)

    layout = tenant_of_row.reshape(blocks, grp_count, own_rows)
    all_tenants = jnp.transpose(layout, (1, 0, 2)).reshape(grp_count, group_rows)
    tenant_hot = all_tenants[:, :, None] == jnp.arange(tenant_count, dtype=jnp.int32)
    all_slots = jnp.sum(jnp.where(tenant_hot, adapter_slot, 0), axis=2)
    mine = all_slots // per_owner == blk_index
    within = jnp.cumsum(mine.astype(jnp.int32), axis=1) - 1
    choose = mine[:, None, :] & (
        within[:, None, :] == jnp.arange(capacity, dtype=jnp.int32)[None, :, None]
    )
    choose_bf = choose.astype(bf16)
    picked_slot = (
        jnp.max(jnp.where(choose, all_slots[:, None, :], -1), axis=2).reshape(1, -1)
    )
    tenants = lax.dynamic_index_in_dim(all_tenants, grp_index, 0, keepdims=False)
    slots = lax.dynamic_index_in_dim(all_slots, grp_index, 0, keepdims=False)
    choose_own = lax.dynamic_index_in_dim(choose_bf, grp_index, 0, keepdims=False)

    slot_of_column = blk_index * per_owner + jnp.arange(per_owner * rank, dtype=jnp.int32) // rank
    slot_mask = slots[:, None] == slot_of_column[None, :]
    tenant_of_column = jnp.arange(tenant_count * rank, dtype=jnp.int32) // rank
    tenant_mask = tenants[:, None] == tenant_of_column[None, :]
    slot_pattern = ranks_pattern(rank, per_owner)
    tenant_pattern = ranks_pattern(rank, tenant_count)

    own_x = dot(choose_own, x).astype(bf16)
    own_dy = dot(choose_own, dy).astype(bf16)
    all_x = lax.all_gather(own_x, "grp", axis=0, tiled=True)
    all_dy = lax.all_gather(own_dy, "grp", axis=0, tiled=True)

    ag = a_gate.reshape(per_owner * rank, width)
    au = a_up.reshape(per_owner * rank, width)
    bd = down_output_factors.reshape(per_owner * rank, width)
    bg = b_gate.reshape(tenant_count * rank, units)
    bu = b_up.reshape(tenant_count * rank, units)
    ad = a_down.reshape(tenant_count * rank, units)

    def select(rows, factors, mask, pattern):
        full = dot(rows, factors, ((1,), (1,)))
        kept = jnp.where(mask, full, 0.0).astype(bf16)
        return dot(pattern, kept, ((1,), (1,)))

    def spread(coeffs, mask, pattern):
        return jnp.where(mask, dot(coeffs, pattern, ((0,), (0,))), 0.0).astype(bf16)

    low_in = jnp.concatenate(
        (
            select(x, ag, slot_mask, slot_pattern),
            select(x, au, slot_mask, slot_pattern),
            adapter_scale * select(dy, bd, slot_mask, slot_pattern),
        ),
        axis=0,
    ).astype(bf16)
    coeffs = sum_over_blk(blocks, low_in, 1)
    p_gate, p_up, grad_q = coeffs[:rank], coeffs[rank : 2 * rank], coeffs[2 * rank :]

    twice = jnp.asarray(adapter_scale, bf16)
    gate_val = dot(x, gate_weight) + dot(spread(twice * p_gate, tenant_mask, tenant_pattern), bg)
    up_val = dot(x, up_weight) + dot(spread(twice * p_up, tenant_mask, tenant_pattern), bu)
    grad_h = dot(dy, down_weight, ((1,), (1,))) + dot(
        spread(grad_q, tenant_mask, tenant_pattern), ad
    )
    act_val, act_slope = silu_pair(gate_val)
    hidden = (act_val * up_val).astype(bf16)
    grad_gate = (grad_h * up_val * act_slope).astype(bf16)
    grad_up = (grad_h * act_val).astype(bf16)

    low_out = jnp.concatenate(
        (
            select(hidden, ad, tenant_mask, tenant_pattern),
            adapter_scale * select(grad_gate, bg, tenant_mask, tenant_pattern),
            adapter_scale * select(grad_up, bu, tenant_mask, tenant_pattern),
        ),
        axis=0,
    ).astype(bf16)
    sums = sum_over_blk(blocks, low_out, 2)
    low_q, dp_gate, dp_up = sums[:rank], sums[rank : 2 * rank], sums[2 * rank :]

    small = jnp.transpose(jnp.concatenate((coeffs, sums), axis=0))
    packed = jnp.concatenate((hidden, grad_gate, grad_up, small), axis=1)
    spare = -packed.shape[1] % 128
    packed = jnp.pad(packed, ((0, 0), (0, spare)))
    everyone = lax.all_gather(packed, "grp", axis=0, tiled=True)

    out_rows = dot(hidden, down_weight) + dot(
        spread(twice * low_q, slot_mask, slot_pattern), bd
    )
    back_in = (
        dot(grad_gate, gate_weight, ((1,), (1,)))
        + dot(grad_up, up_weight, ((1,), (1,)))
        + dot(spread(dp_gate, slot_mask, slot_pattern), ag)
        + dot(spread(dp_up, slot_mask, slot_pattern), au)
    )
    mixed, input_grad = scatter_rows(blocks, out_rows.astype(bf16), back_in.astype(bf16))

    all_small = everyone[:, 3 * units : 3 * units + 6 * rank]
    picked = jnp.einsum(
        "gcn,gnk->gck",
        choose_bf,
        all_small[:, 3 * rank :].reshape(grp_count, group_rows, 3 * rank),
        preferred_element_type=f32,
    ).astype(bf16)
    picked = picked.reshape(grp_count * capacity, 3 * rank)
    slots_dev = per_owner // grp_count
    first_slot = blk_index * per_owner + grp_index * slots_dev
    slot_of_line = first_slot + jnp.arange(slots_dev * rank, dtype=jnp.int32) // rank
    line_mask = slot_of_line[:, None] == picked_slot
    line_pattern = ranks_pattern(rank, slots_dev)

    def slot_grad(values, entries):
        weights = dot(line_pattern, values, ((0,), (1,)))
        weights = jnp.where(line_mask, weights, 0.0).astype(bf16)
        return dot(weights, entries).reshape(slots_dev, rank, width)

    grad_bd = slot_grad(twice * picked[:, :rank], all_dy)
    grad_ag = slot_grad(picked[:, rank : 2 * rank], all_x)
    grad_au = slot_grad(picked[:, 2 * rank :], all_x)

    tenant_dev = tenant_count // grp_count
    tenant_of_line = grp_index * tenant_dev + jnp.arange(tenant_dev * rank, dtype=jnp.int32) // rank
    member = tenant_of_line[:, None] == all_tenants.reshape(1, -1)
    member_pattern = ranks_pattern(rank, tenant_dev)

    def tenant_grad(values, entries):
        weights = dot(member_pattern, values, ((0,), (1,)))
        weights = jnp.where(member, weights, 0.0).astype(bf16)
        return dot(weights, entries).reshape(tenant_dev, rank, units)

    grad_bg = tenant_grad(twice * all_small[:, :rank], everyone[:, units : 2 * units])
    grad_bu = tenant_grad(
        twice * all_small[:, rank : 2 * rank], everyone[:, 2 * units : 3 * units]
    )
    grad_ad = tenant_grad(all_small[:, 2 * rank : 3 * rank], everyone[:, :units])
    return (mixed, input_grad, grad_ag, grad_au, grad_bd, grad_bg, grad_bu, grad_ad)


def solution(mesh):
    placed = (
        P(("blk", "grp"), None),
        P(("blk", "grp"), None),
        P(None, "blk"),
        P(None, "blk"),
        P("blk", None),
        P("blk", None, None),
        P("blk", None, None),
        P("blk", None, None),
        P(None, None, "blk"),
        P(None, None, "blk"),
        P(None, None, "blk"),
        P(),
        P(),
    )
    return jax.shard_map(
        local,
        mesh=mesh,
        in_specs=placed,
        out_specs=(
            P(("blk", "grp"), None),
            P(("blk", "grp"), None),
            P(("blk", "grp"), None, None),
            P(("blk", "grp"), None, None),
            P(("blk", "grp"), None, None),
            P("grp", None, "blk"),
            P("grp", None, "blk"),
            P("grp", None, "blk"),
        ),
        check_vma=False,
    )
```

profile of v0, /device:TPU:0, one launch (start us, length us, event | category | flops | bytes accessed | tf_op | source)
XLA Modules:
  0.0 258.8 jit_solution(8780137954507106174)
XLA Ops:
  7.3 0.8 reshape.184
  8.1 0.1 reshape.185
  8.2 0.9 copy-done.2
  9.1 0.9 copy-done.3
  10.0 51.8 %gather_rows.1 = (bf16[8,16,8192]{2,1,0:T(8,128)(2,1)S(1)}, bf16[8,16,8192]{2,1,0:T(8,128)(2,1)S(1)}) custom-call(bf16[16,8192]{1,0:T(8,128)(2,1)S(1)} %copy-done.2, bf16[16,8192]{1,0:T(8,128)(2,1)S(1)} %copy-done.3), custom_call_target="tpu_custom_call" | custom-call | tf_op jit(solution)/shard_map/gather_rows/pallas_call | solution.py:185
  61.9 1.3 copy-done
  63.2 6.4 %fusion.332 = f32[128,512]{1,0:T(8,128)S(1)} fusion(bf16[128,8192]{1,0:T(8,128)(2,1)S(1)} %bitcast.71, bf16[512,8192]{1,0:T(8,128)(2,1)} %param.17), kind=kOutput, calls=%fused_computation.326 | convolution fusion | flops 1073741824 | bytes 10747904 | tf_op jit(solution)/shard_map/dot_general | solution.py:492
  69.6 0.2 select_reduce_fusion
  69.9 7.1 %fusion.44 = bf16[16,128]{1,0:T(8,128)(2,1)S(1)} fusion(bf16[128,8192]{1,0:T(8,128)(2,1)} %bitcast.72, bf16[512,8192]{1,0:T(8,128)(2,1)} %bitcast.76, s32[512]{0:T(512)S(1)} %get-tuple-element.23, s32[128]{0:T(128)S(1)} %get-tuple-element.22, s32[512]{0:T(512)S(1)} %get-tuple-element.24, s32[512]{0:T(512)S(1)} %fusion.283, pred[512]{0:T(512)(128)(4,1)S(1)} %fusion.286), kind=kOutput, calls=%fused_computation.69 | convolution fusion | flops 1076056064 | bytes 10497024 | tf_op jit(solution)/shard_map/dot_general | solution.py:492
  77.0 6.4 %fusion.46 = bf16[16,128]{1,0:T(8,128)(2,1)S(1)} fusion(bf16[128,8192]{1,0:T(8,128)(2,1)S(1)} %bitcast.66, bf16[512,8192]{1,0:T(8,128)(2,1)} %bitcast.78, s32[512]{0:T(512)S(1)} %get-tuple-element.23, s32[128]{0:T(128)S(1)} %get-tuple-element.22, s32[512]{0:T(512)S(1)} %get-tuple-element.24, s32[512]{0:T(512)S(1)} %fusion.283, pred[512]{0:T(512)(128)(4,1)S(1)} %fusion.286), kind=kOutput, calls=%fused_computation.71 | convolution fusion | flops 1076054016 | bytes 10497024 | tf_op jit(solution)/shard_map/dot_general | solution.py:492
  83.4 6.4 %fusion.45 = bf16[16,128]{1,0:T(8,128)(2,1)S(1)} fusion(bf16[128,8192]{1,0:T(8,128)(2,1)S(1)} %bitcast.67, bf16[512,8192]{1,0:T(8,128)(2,1)} %bitcast.80, s32[512]{0:T(512)S(1)} %get-tuple-element.23, s32[128]{0:T(128)S(1)} %get-tuple-element.22, s32[512]{0:T(512)S(1)} %get-tuple-element.24, s32[512]{0:T(512)S(1)} %fusion.283, pred[512]{0:T(512)(128)(4,1)S(1)} %fusion.286), kind=kOutput, calls=%fused_computation.70 | convolution fusion | flops 1076054016 | bytes 10497024 | tf_op jit(solution)/shard_map/dot_general | solution.py:492
  89.8 6.6 %sum_over_blk.2 = bf16[48,128]{1,0:T(8,128)(2,1)S(1)} custom-call(bf16[48,128]{1,0:T(8,128)(2,1)S(1)} %pad_maximum_fusion.c_ref), custom_call_target="tpu_custom_call" | custom-call | tf_op jit(solution)/shard_map/sum_over_blk/pallas_call | solution.py:466
  96.5 4.6 %fusion.330 = f32[128,512]{1,0:T(8,128)S(1)} fusion(bf16[128,8192]{1,0:T(8,128)(2,1)S(1)} %bitcast.68, bf16[8192,512]{1,0:T(8,128)(2,1)} %param.16), kind=kOutput, calls=%fused_computation.324 | convolution fusion | flops 1073741824 | bytes 10747904 | tf_op jit(solution)/shard_map/dot_general | solution.py:492
  101.1 4.6 %fusion.329 = f32[128,512]{1,0:T(8,128)S(1)} fusion(bf16[128,8192]{1,0:T(8,128)(2,1)S(1)} %bitcast.69, bf16[8192,512]{1,0:T(8,128)(2,1)} %param.15), kind=kOutput, calls=%fused_computation.323 | convolution fusion | flops 1073741824 | bytes 10747904 | tf_op jit(solution)/shard_map/dot_general | solution.py:492
  105.8 3.2 %fusion.22 = f32[128,512]{1,0:T(8,128)S(1)} fusion(f32[128,512]{1,0:T(8,128)S(1)} %fusion.332, bf16[4096,512]{1,0:T(8,128)(2,1)} %bitcast.94, s32[4096]{0:T(1024)S(1)} %get-tuple-element.26, s32[128]{0:T(128)S(1)} %get-tuple-element.21, s32[4096]{0:T(1024)S(1)} %get-tuple-element.25, s32[4096]{0:T(1024)S(1)} %fusion.184, pred[4096]{0:T(1024)(128)(4,1)S(1)} %fusion.187, ...), kind=kOutput, calls=%fused_computation.40 | convolution fusion | flops 555417600 | bytes 4776448 | tf_op jit(solution)/shard_map/dot_general | solution.py:492
  109.0 3.4 %fusion.21 = f32[128,512]{1,0:T(8,128)S(1)} fusion(f32[128,512]{1,0:T(8,128)S(1)} %fusion.330, bf16[4096,512]{1,0:T(8,128)(2,1)} %bitcast.90, s32[4096]{0:T(1024)S(1)} %get-tuple-element.26, s32[128]{0:T(128)S(1)} %get-tuple-element.21, s32[4096]{0:T(1024)S(1)} %get-tuple-element.25, s32[4096]{0:T(1024)S(1)} %fusion.184, pred[4096]{0:T(1024)(128)(4,1)S(1)} %fusion.187, ...), kind=kOutput, calls=%fused_computation.39 | convolution fusion | flops 555419648 | bytes 4776448 | tf_op jit(solution)/shard_map/dot_general | solution.py:492
  112.3 3.3 %multiply_convert_fusion.1 = (bf16[128,512]{1,0:T(8,128)(2,1)S(1)}, bf16[128,512]{1,0:T(8,128)(2,1)S(1)}, bf16[128,512]{1,0:T(8,128)(2,1)S(1)}) fusion(f32[128,512]{1,0:T(8,128)S(1)} %fusion.22, f32[128,512]{1,0:T(8,128)S(1)} %fusion.21, f32[128,512]{1,0:T(8,128)S(1)} %fusion.329, bf16[4096,512]{1,0:T(8,128)(2,1)} %bitcast.92, ...), kind=kOutput, calls=%fused_computation.119 | convolution fusion | flops 556402688 | bytes 5431808 | tf_op jit(solution)/shard_map/dot_general | solution.py:492
  115.7 4.0 %fusion.41 = bf16[16,128]{1,0:T(8,128)(2,1)S(1)} fusion(bf16[128,512]{1,0:T(8,128)(2,1)S(1)} %get-tuple-element.19, bf16[4096,512]{1,0:T(8,128)(2,1)} %bitcast.91, s32[4096]{0:T(1024)S(1)} %get-tuple-element.26, s32[128]{0:T(128)S(1)} %get-tuple-element.21, s32[4096]{0:T(1024)S(1)} %get-tuple-element.25, s32[4096]{0:T(1024)S(1)} %fusion.184, ...), kind=kOutput, calls=%fused_computation.66 | convolution fusion | flops 555356160 | bytes 4383232 | tf_op jit(solution)/shard_map/dot_general | solution.py:492
  119.7 4.0 %fusion.42 = bf16[16,128]{1,0:T(8,128)(2,1)S(1)} fusion(bf16[128,512]{1,0:T(8,128)(2,1)S(1)} %get-tuple-element.18, bf16[4096,512]{1,0:T(8,128)(2,1)} %bitcast.93, s32[4096]{0:T(1024)S(1)} %get-tuple-element.26, s32[128]{0:T(128)S(1)} %get-tuple-element.21, s32[4096]{0:T(1024)S(1)} %get-tuple-element.25, s32[4096]{0:T(1024)S(1)} %fusion.184, ...), kind=kOutput, calls=%fused_computation.67 | convolution fusion | flops 555356160 | bytes 4383232 | tf_op jit(solution)/shard_map/dot_general | solution.py:492
  123.8 4.0 %fusion.43 = bf16[16,128]{1,0:T(8,128)(2,1)S(1)} fusion(bf16[128,512]{1,0:T(8,128)(2,1)S(1)} %get-tuple-element.20, bf16[4096,512]{1,0:T(8,128)(2,1)} %bitcast.95, s32[4096]{0:T(1024)S(1)} %get-tuple-element.26, s32[128]{0:T(128)S(1)} %get-tuple-element.21, s32[4096]{0:T(1024)S(1)} %get-tuple-element.25, s32[4096]{0:T(1024)S(1)} %fusion.184, ...), kind=kOutput, calls=%fused_computation.68 | convolution fusion | flops 555354112 | bytes 4383232 | tf_op jit(solution)/shard_map/dot_general | solution.py:492
  127.8 6.7 %sum_over_blk.3 = bf16[48,128]{1,0:T(8,128)(2,1)S(1)} custom-call(bf16[48,128]{1,0:T(8,128)(2,1)S(1)} %pad_maximum_fusion.1.c_ref), custom_call_target="tpu_custom_call" | custom-call | tf_op jit(solution)/shard_map/sum_over_blk/pallas_call | solution.py:466
  134.5 0.1 copy.30
  134.6 0.8 fusion.89
  135.5 0.3 reduce_window_sum.11
  135.9 1.2 convolution_convert_fusion.1
  137.1 0.0 all-gather.8.cloned.1.call-start
  137.2 2.8 %convolution_convert_fusion = bf16[32,8192]{1,0:T(8,128)(2,1)} fusion(bf16[128,8192]{1,0:T(8,128)(2,1)} %bitcast.73, pred[4,32,128]{2,1,0:T(32,128)(4,1)S(1)} %fusion.145, s32[]{:T(128)S(6)} %select_n.175), kind=kOutput, calls=%fused_computation.6 | convolution fusion | flops 67371008 | bytes 2625540 | tf_op jit(solution)/shard_map/dot_general | solution.py:492
  140.0 6.9 %fusion.331 = f32[128,8192]{1,0:T(8,128)} fusion(bf16[128,512]{1,0:T(8,128)(2,1)S(1)} %get-tuple-element.20, bf16[512,8192]{1,0:T(8,128)(2,1)} %param.17), kind=kOutput, calls=%fused_computation.325 | convolution fusion | flops 1073741824 | bytes 12713984 | tf_op jit(solution)/shard_map/dot_general | solution.py:492
  147.0 8.3 %fusion.333 = f32[128,8192]{1,0:T(8,128)} fusion(bf16[128,512]{1,0:T(8,128)(2,1)S(1)} %get-tuple-element.18, bf16[8192,512]{1,0:T(8,128)(2,1)} %param.15), kind=kOutput, calls=%fused_computation.327 | convolution fusion | flops 1073741824 | bytes 12713984 | tf_op jit(solution)/shard_map/dot_general | solution.py:492
  155.2 0.1 eq.172
  155.3 6.0 %fusion = bf16[128,8192]{1,0:T(8,128)(2,1)S(1)} fusion(f32[128,8192]{1,0:T(8,128)} %fusion.331, bf16[512,8192]{1,0:T(8,128)(2,1)} %bitcast.77, s32[512]{0:T(512)S(1)} %get-tuple-element.23, s32[128]{0:T(128)S(1)} %get-tuple-element.22, s32[512]{0:T(512)S(1)} %get-tuple-element.24, s32[512]{0:T(512)S(1)} %fusion.283, pred[512]{0:T(512)(128)(4,1)S(1)} %fusion.286, ...), kind=kOutput, calls=%fused_computation.4 | convolution fusion | flops 1078151168 | bytes 14691328 | tf_op jit(solution)/shard_map/dot_general | solution.py:492
  161.3 9.8 %convolution_add_fusion.2 = f32[128,8192]{1,0:T(8,128)} fusion(f32[128,8192]{1,0:T(8,128)} %fusion.333, bf16[128,512]{1,0:T(8,128)(2,1)S(1)} %get-tuple-element.19, bf16[8192,512]{1,0:T(8,128)(2,1)} %param.16), kind=kOutput, calls=%fused_computation.2 | convolution fusion | flops 1074790400 | bytes 16908288 | tf_op jit(solution)/shard_map/dot_general | solution.py:492
  171.1 8.1 %convolution_add_fusion.1 = f32[128,8192]{1,0:T(8,128)} fusion(f32[128,8192]{1,0:T(8,128)} %convolution_add_fusion.2, bf16[512,8192]{1,0:T(8,128)(2,1)} %bitcast.81, s32[512]{0:T(512)S(1)} %get-tuple-element.23, s32[128]{0:T(128)S(1)} %get-tuple-element.22, s32[512]{0:T(512)S(1)} %get-tuple-element.24, s32[512]{0:T(512)S(1)} %fusion.283, ...), kind=kOutput, calls=%fused_computation.1 | convolution fusion | flops 1077100544 | bytes 16788480 | tf_op jit(solution)/shard_map/dot_general | solution.py:492
  179.2 7.4 %fusion.1 = bf16[128,8192]{1,0:T(8,128)(2,1)} fusion(f32[128,8192]{1,0:T(8,128)} %convolution_add_fusion.1, bf16[512,8192]{1,0:T(8,128)(2,1)} %bitcast.79, s32[512]{0:T(512)S(1)} %get-tuple-element.23, s32[128]{0:T(128)S(1)} %get-tuple-element.22, s32[512]{0:T(512)S(1)} %get-tuple-element.24, s32[512]{0:T(512)S(1)} %fusion.283, ...), kind=kOutput, calls=%fused_computation.5 | convolution fusion | flops 1078149120 | bytes 14691328 | tf_op jit(solution)/shard_map/dot_general | solution.py:492
  186.6 1.6 copy-done.1
  188.1 40.8 %scatter_rows.1 = (bf16[16,8192]{1,0:T(8,128)(2,1)S(1)}, bf16[16,8192]{1,0:T(8,128)(2,1)S(1)}) custom-call(bf16[8,16,8192]{2,1,0:T(8,128)(2,1)S(1)} %bitcast.74, bf16[8,16,8192]{2,1,0:T(8,128)(2,1)S(1)} %bitcast.75), custom_call_target="tpu_custom_call" | custom-call | tf_op jit(solution)/shard_map/scatter_rows/pallas_call | solution.py:414
  228.9 0.1 select_reduce_fusion.1
  229.1 0.1 eq.167
  229.2 1.0 slice.69
  230.2 0.1 convolution_convert_fusion.2
  230.4 3.6 %fusion.13 = f32[1024,512]{1,0:T(8,128)} fusion(s32[512]{0:T(512)S(1)} %eq.172, s32[1024]{0:T(1024)S(1)} %fusion.235, bf16[512,1664]{1,0:T(8,128)(2,1)} %all-gather.4.cloned.1.call-done, s32[1024]{0:T(1024)S(1)} %get-tuple-element.29, s32[1024]{0:T(1024)S(1)} %get-tuple-element.30, pred[1024]{0:T(1024)(128)(4,1)S(1)} %fusion.233), kind=kOutput, calls=%fused_computation.28 | convolution fusion | flops 555278336 | bytes 2767872 | tf_op jit(solution)/shard_map/dot_general | solution.py:492
  234.0 2.4 fusion.12
  236.3 2.4 fusion.11
  238.7 4.7 %fusion.37 = f32[128,8192]{1,0:T(8,128)} fusion(bf16[128,8192]{1,0:T(8,128)(2,1)} %all-gather.6.cloned.1.call-done, bf16[128,48]{1,0:T(8,128)(2,1)S(1)} %bitcast.85, s32[128]{0:T(128)S(1)} %eq.167, s32[128]{0:T(128)S(1)} %get-tuple-element.28, s32[128]{0:T(128)S(1)} %get-tuple-element.27, s32[128]{0:T(128)S(1)} %broadcast_add_fusion.1, ...), kind=kOutput, calls=%fused_computation.62 | convolution fusion | flops 269015040 | bytes 6305920 | tf_op jit(solution)/shard_map/dot_general | solution.py:492
  243.4 2.9 %fusion.36 = f32[128,8192]{1,0:T(8,128)} fusion(bf16[128,8192]{1,0:T(8,128)(2,1)S(1)} %copy-done.4, bf16[128,48]{1,0:T(8,128)(2,1)S(1)} %bitcast.86, s32[128]{0:T(128)S(1)} %eq.167, s32[128]{0:T(128)S(1)} %get-tuple-element.28, s32[128]{0:T(128)S(1)} %get-tuple-element.27, s32[128]{0:T(128)S(1)} %broadcast_add_fusion.1, pred[128]{0:T(512)(128)(4,1)S(1)} %compare_and_fusion), kind=kOutput, calls=%fused_computation.61 | convolution fusion | flops 269015040 | bytes 6305920 | tf_op jit(solution)/shard_map/dot_general | solution.py:492
  246.4 4.5 %fusion.35 = f32[128,8192]{1,0:T(8,128)} fusion(bf16[128,8192]{1,0:T(8,128)(2,1)} %all-gather.8.cloned.1.call-done, bf16[128,48]{1,0:T(8,128)(2,1)S(1)} %bitcast.87, s32[128]{0:T(128)S(1)} %eq.167, s32[128]{0:T(128)S(1)} %get-tuple-element.28, s32[128]{0:T(128)S(1)} %get-tuple-element.27, s32[128]{0:T(128)S(1)} %broadcast_add_fusion.1, ...), kind=kOutput, calls=%fused_computation.60 | convolution fusion | flops 269017088 | bytes 6305920 | tf_op jit(solution)/shard_map/dot_general | solution.py:492
  250.8 0.7 copy.39
  251.5 0.7 copy.40
  (38 shorter events, 0.3 us)
Async XLA Ops:
  7.2 222.0 %all-gather.4.cloned.1.call-start = ((), (), s32[]{:S(2)}) async-start(), calls=%async_computation | async-start | bytes 2129920 | tf_op jit(solution)/shard_map/all_gather | solution.py:608
  8.1 1.0 copy-start.2
  9.1 0.9 copy-start.3
  61.9 1.3 copy-start
  63.2 6.4 %copy-start.6 = (s32[256]{0:T(256)S(1)}, s32[256]{0:T(256)}, u32[]{:S(2)}) copy-start(s32[256]{0:T(256)} %param.25) | copy-start | bytes 3076
  135.5 103.3 %all-gather.6.cloned.1.call-start = ((), (), s32[]{:S(2)}) async-start(), calls=%async_computation.1 | async-start | bytes 2621440 | tf_op jit(solution)/shard_map/all_gather | solution.py:553
  137.1 109.2 %all-gather.8.cloned.1.call-start = ((), (), s32[]{:S(2)}) async-start(), calls=%async_computation.2 | async-start | bytes 2621440 | tf_op jit(solution)/shard_map/all_gather | solution.py:554
  186.6 1.6 copy-start.1
  230.2 3.7 %copy-start.5 = (bf16[512,1664]{1,0:T(8,128)(2,1)S(1)}, bf16[512,1664]{1,0:T(8,128)(2,1)}, u32[]{:S(2)}) copy-start(bf16[512,1664]{1,0:T(8,128)(2,1)} %all-gather.4.cloned.1.call-done) | copy-start | bytes 5111812
  238.7 4.7 %copy-start.4 = (bf16[128,8192]{1,0:T(8,128)(2,1)S(1)}, bf16[128,8192]{1,0:T(8,128)(2,1)}, u32[]{:S(2)}) copy-start(bf16[128,8192]{1,0:T(8,128)(2,1)} %all-gather.6.cloned.1.call-done) | copy-start | bytes 6291460
Sparse Core Ops, SparseCore 0:
  135.6 20.6 all-gather.3
  158.4 22.5 all-gather.5
  182.6 22.5 all-gather.7
where the time goes:
time: 260 us; the launch traced here: 259 us
  matrix products  129 us (50%)
  Pallas kernels  106 us (41%)
  between operations  14 us (5%)
  local copies, waits for them, and re-layouts  8.36 us (3%)
    dot_general x26, matrix products, dot(): return lax.dot_general(a, b, (dims, ((), ())), preferred_element_type=f32)  129 us
    pallas_call x1, Pallas kernels, gather_rows(): pl.pallas_call(functools.partial(gather_kernel, blocks), out_shape=(shape...  51.8 us
    pallas_call x1, Pallas kernels, scatter_rows(): pl.pallas_call(functools.partial(scatter_kernel, blocks), out_shape=(bloc...  40.8 us
    pallas_call x2, Pallas kernels, sum_over_blk(): pl.pallas_call(functools.partial(sum_kernel, blocks), out_shape=jax.Shape...  13.3 us
    unnamed x16, local copies, waits for them, and re-layouts  6.22 us
  transfers between devices with their start and end apart: 3, of which 0 were waited for; matrix products, arithmetic and copies ran while one was open for 26% of the time, Pallas kernels for 16%

commit v1 on v0

--- a/solution.py
+++ b/solution.py
@@ -185,7 +185,7 @@
     got = pl.pallas_call(
         functools.partial(gather_kernel, blocks),
         out_shape=(shape, shape),
-        in_specs=[pl.BlockSpec(memory_space=pltpu.VMEM)] * 2,
+        in_specs=[pl.BlockSpec(memory_space=pl.ANY)] * 2,
         out_specs=(pl.BlockSpec(memory_space=pl.ANY),) * 2,
         scratch_shapes=[dma((2,))] + [dma((2, line))] * 6 + [dma((2,))] * 2,
         compiler_params=pltpu.CompilerParams(
@@ -498,6 +498,206 @@
     return (column % rank == row).astype(bf16)
 
 
+def lanes_entry(rank, first, count):
+    return (lax.broadcasted_iota(jnp.int32, (1, count), 1) // rank) + first
+
+
+def spread_kernel(coeffs, mask, pattern):
+    return jnp.where(mask, dot(coeffs, pattern), 0.0).astype(bf16)
+
+
+def select_kernel(full, mask, pattern):
+    kept = jnp.where(mask, full, 0.0).astype(bf16)
+    return dot(pattern, kept, ((1,), (1,)))
+
+
+def inputs_kernel(
+    rank, x, d, gw, uw, dw, ag, au, bd, slot, pat, gate_o, up_o, gh_o, low_o, qg, qu, qd
+):
+    step = pl.program_id(0)
+    xv, dv = x[...], d[...]
+    terms = (
+        (gate_o, lambda: dot(xv, gw[...])),
+        (up_o, lambda: dot(xv, uw[...])),
+        (gh_o, lambda: dot(dv, dw[...], ((1,), (1,)))),
+        (qg, lambda: dot(xv, ag[...], ((1,), (1,)))),
+        (qu, lambda: dot(xv, au[...], ((1,), (1,)))),
+        (qd, lambda: dot(dv, bd[...], ((1,), (1,)))),
+    )
+
+    @pl.when(step == 0)
+    def _():
+        for ref, _term in terms:
+            ref[...] = jnp.zeros_like(ref)
+
+    for ref, term in terms:
+        ref[...] += term()
+
+    @pl.when(step == pl.num_programs(0) - 1)
+    def _():
+        mask = slot[...] == lanes_entry(rank, 0, qg.shape[1])
+        for k, (ref, scale) in enumerate(((qg, 1.0), (qu, 1.0), (qd, adapter_scale))):
+            low_o[k * rank : (k + 1) * rank, :] = (
+                scale * select_kernel(ref[...], mask, pat[...])
+            ).astype(bf16)
+
+
+def input_terms(rank, x, dy, gw, uw, dw, ag, au, bd, slot, pat):
+    rows, width = x.shape
+    units, own = gw.shape[1], ag.shape[0]
+    tile = min(512, width)
+    across = lambda n: pl.BlockSpec((n, tile), lambda i: (0, i))
+    down = lambda n: pl.BlockSpec((tile, n), lambda i: (i, 0))
+    whole = lambda *shape: pl.BlockSpec(shape, lambda i: (0, 0))
+    acc = jax.ShapeDtypeStruct((rows, units), f32)
+    return pl.pallas_call(
+        functools.partial(inputs_kernel, rank),
+        grid=(width // tile,),
+        out_shape=(acc, acc, acc, jax.ShapeDtypeStruct((3 * rank, rows), bf16)),
+        in_specs=[
+            across(rows),
+            across(rows),
+            down(units),
+            down(units),
+            across(units),
+            across(own),
+            across(own),
+            across(own),
+            whole(rows, 1),
+            whole(*pat.shape),
+        ],
+        out_specs=(whole(rows, units),) * 3 + (whole(3 * rank, rows),),
+        scratch_shapes=[pltpu.VMEM((rows, own), f32)] * 3,
+        compiler_params=pltpu.CompilerParams(vmem_limit_bytes=32 * 2**20),
+        cost_estimate=pl.CostEstimate(
+            flops=6 * rows * width * (units + own),
+            bytes_accessed=6 * width * (units + own),
+            transcendentals=0,
+        ),
+        name="input_terms",
+    )(x, dy, gw, uw, dw, ag, au, bd, slot, pat)
+
+
+def middle_kernel(
+    rank, gate, up, gh, coeffs, tenant, pat, bg, bu, ad, hid_o, gg_o, gu_o, low_o, sg, su, sh, low
+):
+    half, step = pl.program_id(0), pl.program_id(1)
+    last = pl.num_programs(1) - 1
+    count = bg.shape[0]
+    mask = tenant[...] == lanes_entry(rank, step * (count // rank), count)
+
+    @pl.when((half == 0) & (step == 0))
+    def _():
+        sg[...] = gate[...]
+        su[...] = up[...]
+        sh[...] = gh[...]
+
+    @pl.when(half == 0)
+    def _():
+        for k, (acc, fac, scale) in enumerate(
+            ((sg, bg, adapter_scale), (su, bu, adapter_scale), (sh, ad, 1.0))
+        ):
+            given = coeffs[:, k * rank : (k + 1) * rank]
+            acc[...] += scale * dot(spread_kernel(given, mask, pat[...]), fac[...])
+
+    @pl.when((half == 0) & (step == last))
+    def _():
+        act_val, act_slope = silu_pair(sg[...])
+        up_val, grad_h = su[...], sh[...]
+        hid_o[...] = (act_val * up_val).astype(bf16)
+        gg_o[...] = (grad_h * up_val * act_slope).astype(bf16)
+        gu_o[...] = (grad_h * act_val).astype(bf16)
+        low[...] = jnp.zeros_like(low)
+
+    @pl.when(half == 1)
+    def _():
+        for k, (rows, fac, scale) in enumerate(
+            ((hid_o, ad, 1.0), (gg_o, bg, adapter_scale), (gu_o, bu, adapter_scale))
+        ):
+            full = dot(rows[...], fac[...], ((1,), (1,)))
+            low[k * rank : (k + 1) * rank, :] += scale * select_kernel(full, mask, pat[...])
+
+    @pl.when((half == 1) & (step == last))
+    def _():
+        low_o[...] = low[...].astype(bf16)
+
+
+def middle_terms(rank, gate, up, gh, coeffs, tenant, bg, bu, ad):
+    rows, units = gate.shape
+    total = bg.shape[0]
+    tile = min(1024, total)
+    pat = ranks_pattern(rank, tile // rank)
+    whole = lambda *shape: pl.BlockSpec(shape, lambda h, i: (0, 0))
+    down = pl.BlockSpec((tile, units), lambda h, i: (i, 0))
+    block = jax.ShapeDtypeStruct((rows, units), bf16)
+    return pl.pallas_call(
+        functools.partial(middle_kernel, rank),
+        grid=(2, total // tile),
+        out_shape=(block, block, block, jax.ShapeDtypeStruct((3 * rank, rows), bf16)),
+        in_specs=[whole(rows, units)] * 3
+        + [whole(rows, 3 * rank), whole(rows, 1), whole(*pat.shape)]
+        + [down] * 3,
+        out_specs=(whole(rows, units),) * 3 + (whole(3 * rank, rows),),
+        scratch_shapes=[pltpu.VMEM((rows, units), f32)] * 3
+        + [pltpu.VMEM((3 * rank, rows), f32)],
+        compiler_params=pltpu.CompilerParams(vmem_limit_bytes=32 * 2**20),
+        cost_estimate=pl.CostEstimate(
+            flops=12 * rows * total * units,
+            bytes_accessed=12 * total * units,
+            transcendentals=rows * units,
+        ),
+        name="middle_terms",
+    )(gate, up, gh, coeffs, tenant, pat, bg, bu, ad)
+
+
+def outputs_kernel(
+    rank, hid, gg, gu, sums, slot, pat, gw, uw, dw, ag, au, bd, mixed_o, back_o, eq, eg, eu
+):
+    @pl.when(pl.program_id(0) == 0)
+    def _():
+        mask = slot[...] == lanes_entry(rank, 0, eq.shape[1])
+        for k, (ref, scale) in enumerate(((eq, adapter_scale), (eg, 1.0), (eu, 1.0))):
+            given = sums[:, k * rank : (k + 1) * rank]
+            ref[...] = (
+                scale * jnp.where(mask, dot(given, pat[...]), 0.0)
+            ).astype(bf16)
+
+    mixed_o[...] = (dot(hid[...], dw[...]) + dot(eq[...], bd[...])).astype(bf16)
+    back_o[...] = (
+        dot(gg[...], gw[...], ((1,), (1,)))
+        + dot(gu[...], uw[...], ((1,), (1,)))
+        + dot(eg[...], ag[...])
+        + dot(eu[...], au[...])
+    ).astype(bf16)
+
+
+def output_terms(rank, hid, gg, gu, sums, slot, pat, gw, uw, dw, ag, au, bd):
+    rows, units = hid.shape
+    width, own = ag.shape[1], ag.shape[0]
+    tile = min(512, width)
+    across = lambda n: pl.BlockSpec((n, tile), lambda i: (0, i))
+    down = lambda n: pl.BlockSpec((tile, n), lambda i: (i, 0))
+    whole = lambda *shape: pl.BlockSpec(shape, lambda i: (0, 0))
+    block = jax.ShapeDtypeStruct((rows, width), bf16)
+    return pl.pallas_call(
+        functools.partial(outputs_kernel, rank),
+        grid=(width // tile,),
+        out_shape=(block, block),
+        in_specs=[whole(rows, units)] * 3
+        + [whole(rows, 3 * rank), whole(rows, 1), whole(*pat.shape)]
+        + [down(units), down(units), across(units), across(own), across(own), across(own)],
+        out_specs=(across(rows), across(rows)),
+        scratch_shapes=[pltpu.VMEM((rows, own), bf16)] * 3,
+        compiler_params=pltpu.CompilerParams(vmem_limit_bytes=32 * 2**20),
+        cost_estimate=pl.CostEstimate(
+            flops=6 * rows * width * (units + own),
+            bytes_accessed=6 * width * (units + own),
+            transcendentals=0,
+        ),
+        name="output_terms",
+    )(hid, gg, gu, sums, slot, pat, gw, uw, dw, ag, au, bd)
+
+
 def local(
     tokens,
     cotangent,
@@ -541,17 +741,11 @@
     slots = lax.dynamic_index_in_dim(all_slots, grp_index, 0, keepdims=False)
     choose_own = lax.dynamic_index_in_dim(choose_bf, grp_index, 0, keepdims=False)
 
-    slot_of_column = blk_index * per_owner + jnp.arange(per_owner * rank, dtype=jnp.int32) // rank
-    slot_mask = slots[:, None] == slot_of_column[None, :]
-    tenant_of_column = jnp.arange(tenant_count * rank, dtype=jnp.int32) // rank
-    tenant_mask = tenants[:, None] == tenant_of_column[None, :]
+    local_slot = (slots - blk_index * per_owner)[:, None]
     slot_pattern = ranks_pattern(rank, per_owner)
-    tenant_pattern = ranks_pattern(rank, tenant_count)
 
     own_x = dot(choose_own, x).astype(bf16)
     own_dy = dot(choose_own, dy).astype(bf16)
-    all_x = lax.all_gather(own_x, "grp", axis=0, tiled=True)
-    all_dy = lax.all_gather(own_dy, "grp", axis=0, tiled=True)
 
     ag = a_gate.reshape(per_owner * rank, width)
     au = a_up.reshape(per_owner * rank, width)
@@ -560,63 +754,40 @@
     bu = b_up.reshape(tenant_count * rank, units)
     ad = a_down.reshape(tenant_count * rank, units)
 
-    def select(rows, factors, mask, pattern):
-        full = dot(rows, factors, ((1,), (1,)))
-        kept = jnp.where(mask, full, 0.0).astype(bf16)
-        return dot(pattern, kept, ((1,), (1,)))
-
-    def spread(coeffs, mask, pattern):
-        return jnp.where(mask, dot(coeffs, pattern, ((0,), (0,))), 0.0).astype(bf16)
-
-    low_in = jnp.concatenate(
-        (
-            select(x, ag, slot_mask, slot_pattern),
-            select(x, au, slot_mask, slot_pattern),
-            adapter_scale * select(dy, bd, slot_mask, slot_pattern),
-        ),
-        axis=0,
-    ).astype(bf16)
-    coeffs = sum_over_blk(blocks, low_in, 1)
-    p_gate, p_up, grad_q = coeffs[:rank], coeffs[rank : 2 * rank], coeffs[2 * rank :]
-
+    gate_in, up_in, grad_in, low_in = input_terms(
+        rank, x, dy, gate_weight, up_weight, down_weight, ag, au, bd, local_slot, slot_pattern
+    )
+    low_in, own_x, own_dy = lax.optimization_barrier((low_in, own_x, own_dy))
+    all_x = lax.all_gather(own_x, "grp", axis=0, tiled=True)
+    all_dy = lax.all_gather(own_dy, "grp", axis=0, tiled=True)
     twice = jnp.asarray(adapter_scale, bf16)
-    gate_val = dot(x, gate_weight) + dot(spread(twice * p_gate, tenant_mask, tenant_pattern), bg)
-    up_val = dot(x, up_weight) + dot(spread(twice * p_up, tenant_mask, tenant_pattern), bu)
-    grad_h = dot(dy, down_weight, ((1,), (1,))) + dot(
-        spread(grad_q, tenant_mask, tenant_pattern), ad
-    )
-    act_val, act_slope = silu_pair(gate_val)
-    hidden = (act_val * up_val).astype(bf16)
-    grad_gate = (grad_h * up_val * act_slope).astype(bf16)
-    grad_up = (grad_h * act_val).astype(bf16)
-
-    low_out = jnp.concatenate(
-        (
-            select(hidden, ad, tenant_mask, tenant_pattern),
-            adapter_scale * select(grad_gate, bg, tenant_mask, tenant_pattern),
-            adapter_scale * select(grad_up, bu, tenant_mask, tenant_pattern),
-        ),
-        axis=0,
-    ).astype(bf16)
-    sums = sum_over_blk(blocks, low_out, 2)
-    low_q, dp_gate, dp_up = sums[:rank], sums[rank : 2 * rank], sums[2 * rank :]
-
-    small = jnp.transpose(jnp.concatenate((coeffs, sums), axis=0))
-    packed = jnp.concatenate((hidden, grad_gate, grad_up, small), axis=1)
+    coeffs = jnp.transpose(sum_over_blk(blocks, low_in, 1))
+    hidden, grad_gate, grad_up, low_out = middle_terms(
+        rank, gate_in, up_in, grad_in, coeffs, tenants[:, None], bg, bu, ad
+    )
+    sums = jnp.transpose(sum_over_blk(blocks, low_out, 2))
+
+    packed = jnp.concatenate((hidden, grad_gate, grad_up, coeffs, sums), axis=1)
     spare = -packed.shape[1] % 128
     packed = jnp.pad(packed, ((0, 0), (0, spare)))
     everyone = lax.all_gather(packed, "grp", axis=0, tiled=True)
 
-    out_rows = dot(hidden, down_weight) + dot(
-        spread(twice * low_q, slot_mask, slot_pattern), bd
-    )
-    back_in = (
-        dot(grad_gate, gate_weight, ((1,), (1,)))
-        + dot(grad_up, up_weight, ((1,), (1,)))
-        + dot(spread(dp_gate, slot_mask, slot_pattern), ag)
-        + dot(spread(dp_up, slot_mask, slot_pattern), au)
-    )
-    mixed, input_grad = scatter_rows(blocks, out_rows.astype(bf16), back_in.astype(bf16))
+    mixed_terms, back_terms = output_terms(
+        rank,
+        hidden,
+        grad_gate,
+        grad_up,
+        sums,
+        local_slot,
+        slot_pattern,
+        gate_weight,
+        up_weight,
+        down_weight,
+        ag,
+        au,
+        bd,
+    )
+    mixed, input_grad = scatter_rows(blocks, mixed_terms, back_terms)
 
     all_small = everyone[:, 3 * units : 3 * units + 6 * rank]
     picked = jnp.einsum(

time: 260 us -> 233 us (0.90)
  matrix products: 129 us -> 24.6 us
  Pallas kernels: 106 us -> 160 us
  local copies, waits for them, and re-layouts: 8.36 us -> 30.1 us
    dot_general x26 -> x8, matrix products: 129 us -> 24.4 us  [dot(): return lax.dot_general(a, b, (dims, ((), ())), preferred_element_type=f32)]
    pallas_call x0 -> x3, Pallas kernels: none -> 54.2 us  [the longest x1 22.4 us: input_terms(): pl.pallas_call(functools.partial(inputs_kernel, rank), grid=(width // til...]
    unnamed x16 -> x28, local copies, waits for them, and re-layouts: 6.22 us -> 26.7 us
  transfers between devices with their start and end apart: 3 -> 3, of which waited for: 0 -> 0; matrix products, arithmetic and copies ran while one was open for 26% -> 8% of each run, Pallas kernels for 16% -> 26%
where the time goes in v1:
time: 233 us; the launch traced here: 232 us
  Pallas kernels  160 us (69%)
  local copies, waits for them, and re-layouts  30.1 us (13%)
  matrix products  24.6 us (11%)
  between operations  13.9 us (6%)
    pallas_call x1, Pallas kernels, gather_rows(): pl.pallas_call(functools.partial(gather_kernel, blocks), out_shape=(shape...  51.8 us
    pallas_call x1, Pallas kernels, scatter_rows(): pl.pallas_call(functools.partial(scatter_kernel, blocks), out_shape=(bloc...  40.6 us
    unnamed x28, local copies, waits for them, and re-layouts  26.7 us
    dot_general x8, matrix products, dot(): return lax.dot_general(a, b, (dims, ((), ())), preferred_element_type=f32)  24.4 us
    pallas_call x1, Pallas kernels, input_terms(): pl.pallas_call(functools.partial(inputs_kernel, rank), grid=(width // til...  22.4 us
    pallas_call x1, Pallas kernels, output_terms(): pl.pallas_call(functools.partial(outputs_kernel, rank), grid=(width // ti...  20.7 us
    pallas_call x2, Pallas kernels, sum_over_blk(): pl.pallas_call(functools.partial(sum_kernel, blocks), out_shape=jax.Shape...  13.3 us
    pallas_call x1, Pallas kernels, middle_terms(): pl.pallas_call(functools.partial(middle_kernel, rank), grid=(2, total //...  11 us
  transfers between devices with their start and end apart: 3, of which 0 were waited for; matrix products, arithmetic and copies ran while one was open for 8% of the time, Pallas kernels for 26%

profile of v1, /device:TPU:0, one launch (start us, length us, event | category | flops | bytes accessed | tf_op | source)
XLA Modules:
  0.0 231.6 jit_solution(12460416760373058140)
XLA Ops:
  7.2 0.0 all-gather.4.cloned.1.call-start
  7.3 0.8 reshape.168
  8.0 0.1 eq.101
  8.1 0.9 select_reduce_fusion
  9.1 0.1 copy.42.slot
  9.2 0.3 reduce_window_sum.11
  9.5 0.9 copy-done.9
  10.5 0.9 copy-done.10
  11.4 51.8 %gather_rows.1 = (bf16[8,16,8192]{2,1,0:T(8,128)(2,1)S(1)}, bf16[8,16,8192]{2,1,0:T(8,128)(2,1)S(1)}) custom-call(bf16[16,8192]{1,0:T(8,128)(2,1)S(1)} %copy-done.9, bf16[16,8192]{1,0:T(8,128)(2,1)S(1)} %copy-done.10), custom_call_target="tpu_custom_call" | custom-call | tf_op jit(solution)/shard_map/gather_rows/pallas_call | solution.py:185
  63.2 1.3 copy-done.4
  64.6 1.2 convolution_convert_fusion.1
  65.8 2.8 %convolution_convert_fusion = bf16[32,8192]{1,0:T(8,128)(2,1)} fusion(bf16[128,8192]{1,0:T(8,128)(2,1)} %bitcast.38, pred[4,32,128]{2,1,0:T(32,128)(4,1)S(1)} %fusion.33, s32[]{:T(128)S(6)} %select_n.100), kind=kOutput, calls=%fused_computation | convolution fusion | flops 67371008 | bytes 2625540 | tf_op jit(solution)/shard_map/dot_general | solution.py:492
  68.6 3.4 %copy-done = bf16[8192,512]{1,0:T(8,128)(2,1)S(1)} copy-done((bf16[8192,512]{1,0:T(8,128)(2,1)S(1)}, bf16[8192,512]{1,0:T(8,128)(2,1)}, u32[]{:S(2)}) %copy-start) | copy-done | bytes 8388632
  72.0 3.4 %copy-done.2 = bf16[8192,512]{1,0:T(8,128)(2,1)S(1)} copy-done((bf16[8192,512]{1,0:T(8,128)(2,1)S(1)}, bf16[8192,512]{1,0:T(8,128)(2,1)}, u32[]{:S(2)}) %copy-start.2) | copy-done | bytes 8388632
  75.4 1.6 copy-done.5
  77.0 22.4 %input_terms.1 = (f32[128,512]{1,0:T(8,128)S(1)}, f32[128,512]{1,0:T(8,128)S(1)}, f32[128,512]{1,0:T(8,128)S(1)}, bf16[48,128]{1,0:T(8,128)(2,1)S(1)}) custom-call(bf16[128,8192]{1,0:T(8,128)(2,1)S(1)} %bitcast.37, bf16[128,8192]{1,0:T(8,128)(2,1)S(1)} %bitcast.39, bf16[8192,512]{1,0:T(8,128)(2,1)S(1)} %copy-done, bf16[8192,512]{1,0:T(8,128)(2,1)S(1)} %copy-done.2, ...), custom_call_target="tpu_custom_call" | custom-call | flops 6442450944 | bytes 50331648 | tf_op jit(solution)/shard_map/input_terms/pallas_call | solution.py:553
  99.4 6.6 %sum_over_blk.2 = bf16[48,128]{1,0:T(8,128)(2,1)S(1)} custom-call(bf16[48,128]{1,0:T(8,128)(2,1)S(1)} %get-tuple-element.31.c_ref), custom_call_target="tpu_custom_call" | custom-call | tf_op jit(solution)/shard_map/sum_over_blk/pallas_call | solution.py:466
  106.0 0.1 copy.43
  106.2 0.1 copy.44.tenant
  106.3 2.2 copy-done.6
  108.5 2.2 copy-done.7
  110.7 2.2 copy-done.8
  112.9 11.0 %middle_terms.1 = (bf16[128,512]{1,0:T(8,128)(2,1)S(1)}, bf16[128,512]{1,0:T(8,128)(2,1)S(1)}, bf16[128,512]{1,0:T(8,128)(2,1)S(1)}, bf16[48,128]{1,0:T(8,128)(2,1)S(1)}) custom-call(f32[128,512]{1,0:T(8,128)S(1)} %get-tuple-element.27.gate, f32[128,512]{1,0:T(8,128)S(1)} %get-tuple-element.28.up, f32[128,512]{1,0:T(8,128)S(1)} %get-tuple-element.29.gh, ...), custom_call_target="tpu_custom_call" | custom-call | flops 3221225472 | bytes 25165824 | tf_op jit(solution)/shard_map/middle_terms/pallas_call | solution.py:633
  123.9 6.7 %sum_over_blk.3 = bf16[48,128]{1,0:T(8,128)(2,1)S(1)} custom-call(bf16[48,128]{1,0:T(8,128)(2,1)S(1)} %get-tuple-element.35.c_ref), custom_call_target="tpu_custom_call" | custom-call | tf_op jit(solution)/shard_map/sum_over_blk/pallas_call | solution.py:466
  130.6 0.1 copy.45
  130.7 0.1 concatenate.3
  130.9 0.8 pad.4
  131.7 0.0 all-gather.6.cloned.1.call-start
  131.7 0.7 all-gather.6.cloned.1.call-update
  132.4 0.0 all-gather.8.cloned.1.call-start
  132.5 0.7 all-gather.8.cloned.1.call-update
  133.2 0.1 eq.118
  133.3 3.4 %copy-done.1 = bf16[8192,512]{1,0:T(8,128)(2,1)S(1)} copy-done((bf16[8192,512]{1,0:T(8,128)(2,1)S(1)}, bf16[8192,512]{1,0:T(8,128)(2,1)}, u32[]{:S(2)}) %copy-start.1) | copy-done | bytes 8388632
  136.6 3.8 %copy-done.3 = bf16[8192,512]{1,0:T(8,128)(2,1)S(1)} copy-done((bf16[8192,512]{1,0:T(8,128)(2,1)S(1)}, bf16[8192,512]{1,0:T(8,128)(2,1)}, u32[]{:S(2)}) %copy-start.3) | copy-done | bytes 8388632
  140.4 20.7 %output_terms.1 = (bf16[128,8192]{1,0:T(8,128)(2,1)S(1)}, bf16[128,8192]{1,0:T(8,128)(2,1)S(1)}) custom-call(bf16[128,512]{1,0:T(8,128)(2,1)S(1)} %get-tuple-element.32.hid, bf16[128,512]{1,0:T(8,128)(2,1)S(1)} %get-tuple-element.33.gg, bf16[128,512]{1,0:T(8,128)(2,1)S(1)} %get-tuple-element.34.gu, bf16[128,48]{1,0:T(8,128)(2,1)S(1)} %bitcast.46, ...), custom_call_target="tpu_custom_call" | custom-call | flops 6442450944 | bytes 50331648 | tf_op jit(solution)/shard_map/output_terms/pallas_call | solution.py:682
  161.1 40.6 %scatter_rows.1 = (bf16[16,8192]{1,0:T(8,128)(2,1)S(1)}, bf16[16,8192]{1,0:T(8,128)(2,1)S(1)}) custom-call(bf16[8,16,8192]{2,1,0:T(8,128)(2,1)S(1)} %bitcast.43, bf16[8,16,8192]{2,1,0:T(8,128)(2,1)S(1)} %bitcast.44), custom_call_target="tpu_custom_call" | custom-call | tf_op jit(solution)/shard_map/scatter_rows/pallas_call | solution.py:414
  201.7 0.1 select_reduce_fusion.1
  201.9 0.1 eq.113
  202.0 1.0 slice.45
  203.1 0.1 convolution_convert_fusion.2
  203.2 3.6 %fusion.5 = f32[1024,512]{1,0:T(8,128)} fusion(s32[512]{0:T(512)S(1)} %eq.118, s32[1024]{0:T(1024)S(1)} %fusion.63, bf16[512,1664]{1,0:T(8,128)(2,1)} %all-gather.4.cloned.1.call-done, s32[1024]{0:T(1024)S(1)} %get-tuple-element.48, s32[1024]{0:T(1024)S(1)} %get-tuple-element.49, pred[1024]{0:T(1024)(128)(4,1)S(1)} %fusion.80), kind=kOutput, calls=%fused_computation.10 | convolution fusion | flops 555278336 | bytes 2767872 | tf_op jit(solution)/shard_map/dot_general | solution.py:492
  206.8 2.4 %fusion.4 = f32[1024,512]{1,0:T(8,128)} fusion(s32[512]{0:T(512)S(1)} %eq.118, s32[1024]{0:T(1024)S(1)} %fusion.63, bf16[512,1664]{1,0:T(8,128)(2,1)S(1)} %copy-done.12, s32[1024]{0:T(1024)S(1)} %get-tuple-element.48, s32[1024]{0:T(1024)S(1)} %get-tuple-element.49, pred[1024]{0:T(1024)(128)(4,1)S(1)} %fusion.80), kind=kOutput, calls=%fused_computation.9 | convolution fusion | flops 555278336 | bytes 2767872 | tf_op jit(solution)/shard_map/dot_general | solution.py:492
  209.1 2.4 %fusion.3 = f32[1024,512]{1,0:T(8,128)} fusion(s32[512]{0:T(512)S(1)} %eq.118, s32[1024]{0:T(1024)S(1)} %fusion.63, bf16[512,1664]{1,0:T(8,128)(2,1)S(1)} %copy-done.12, s32[1024]{0:T(1024)S(1)} %get-tuple-element.48, s32[1024]{0:T(1024)S(1)} %get-tuple-element.49, pred[1024]{0:T(1024)(128)(4,1)S(1)} %fusion.80), kind=kOutput, calls=%fused_computation.8 | convolution fusion | flops 555270144 | bytes 2767872 | tf_op jit(solution)/shard_map/dot_general | solution.py:492
  211.5 4.7 %fusion.11 = f32[128,8192]{1,0:T(8,128)} fusion(bf16[128,8192]{1,0:T(8,128)(2,1)} %all-gather.6.cloned.1.call-done, bf16[128,48]{1,0:T(8,128)(2,1)S(1)} %bitcast.58, s32[128]{0:T(128)S(1)} %eq.113, s32[128]{0:T(128)S(1)} %get-tuple-element.51, s32[128]{0:T(128)S(1)} %get-tuple-element.50, s32[128]{0:T(128)S(1)} %broadcast_add_fusion.1, ...), kind=kOutput, calls=%fused_computation.20 | convolution fusion | flops 269015040 | bytes 6305920 | tf_op jit(solution)/shard_map/dot_general | solution.py:492
  216.2 2.9 %fusion.10 = f32[128,8192]{1,0:T(8,128)} fusion(bf16[128,8192]{1,0:T(8,128)(2,1)S(1)} %copy-done.11, bf16[128,48]{1,0:T(8,128)(2,1)S(1)} %bitcast.59, s32[128]{0:T(128)S(1)} %eq.113, s32[128]{0:T(128)S(1)} %get-tuple-element.51, s32[128]{0:T(128)S(1)} %get-tuple-element.50, s32[128]{0:T(128)S(1)} %broadcast_add_fusion.1, pred[128]{0:T(512)(128)(4,1)S(1)} %compare_and_fusion), kind=kOutput, calls=%fused_computation.19 | convolution fusion | flops 269015040 | bytes 6305920 | tf_op jit(solution)/shard_map/dot_general | solution.py:492
  219.2 4.5 %fusion.9 = f32[128,8192]{1,0:T(8,128)} fusion(bf16[128,8192]{1,0:T(8,128)(2,1)} %all-gather.8.cloned.1.call-done, bf16[128,48]{1,0:T(8,128)(2,1)S(1)} %bitcast.60, s32[128]{0:T(128)S(1)} %eq.113, s32[128]{0:T(128)S(1)} %get-tuple-element.51, s32[128]{0:T(128)S(1)} %get-tuple-element.50, s32[128]{0:T(128)S(1)} %broadcast_add_fusion.1, ...), kind=kOutput, calls=%fused_computation.18 | convolution fusion | flops 269017088 | bytes 6305920 | tf_op jit(solution)/shard_map/dot_general | solution.py:492
  223.6 0.7 copy.55
  224.3 0.7 copy.56
  (34 shorter events, 0.2 us)
Async XLA Ops:
  7.2 194.9 %all-gather.4.cloned.1.call-start = ((), (), s32[]{:S(2)}) async-start(), calls=%async_computation | async-start | bytes 2129920 | tf_op jit(solution)/shard_map/all_gather | solution.py:773
  9.5 1.0 copy-start.9
  10.5 0.9 copy-start.10
  63.2 1.3 copy-start.4
  68.6 3.4 %copy-start = (bf16[8192,512]{1,0:T(8,128)(2,1)S(1)}, bf16[8192,512]{1,0:T(8,128)(2,1)}, u32[]{:S(2)}) copy-start(bf16[8192,512]{1,0:T(8,128)(2,1)} %gw.3) | copy-start | bytes 25165828
  72.0 3.4 %copy-start.2 = (bf16[8192,512]{1,0:T(8,128)(2,1)S(1)}, bf16[8192,512]{1,0:T(8,128)(2,1)}, u32[]{:S(2)}) copy-start(bf16[8192,512]{1,0:T(8,128)(2,1)} %uw.3) | copy-start | bytes 25165828
  75.4 1.6 copy-start.5
  106.3 2.2 copy-start.6
  108.5 2.2 copy-start.7
  110.7 2.2 copy-start.8
  131.7 79.8 %all-gather.6.cloned.1.call-start = ((), (), s32[]{:S(2)}) async-start(), calls=%async_computation.1 | async-start | bytes 2621440 | tf_op jit(solution)/shard_map/all_gather | solution.py:761
  132.4 86.7 %all-gather.8.cloned.1.call-start = ((), (), s32[]{:S(2)}) async-start(), calls=%async_computation.2 | async-start | bytes 2621440 | tf_op jit(solution)/shard_map/all_gather | solution.py:762
  133.2 3.4 %copy-start.1 = (bf16[8192,512]{1,0:T(8,128)(2,1)S(1)}, bf16[8192,512]{1,0:T(8,128)(2,1)}, u32[]{:S(2)}) copy-start(bf16[8192,512]{1,0:T(8,128)(2,1)} %gw.3) | copy-start | bytes 25165828
  136.6 3.8 %copy-start.3 = (bf16[8192,512]{1,0:T(8,128)(2,1)S(1)}, bf16[8192,512]{1,0:T(8,128)(2,1)}, u32[]{:S(2)}) copy-start(bf16[8192,512]{1,0:T(8,128)(2,1)} %uw.3) | copy-start | bytes 25165828
  203.0 3.7 %copy-start.12 = (bf16[512,1664]{1,0:T(8,128)(2,1)S(1)}, bf16[512,1664]{1,0:T(8,128)(2,1)}, u32[]{:S(2)}) copy-start(bf16[512,1664]{1,0:T(8,128)(2,1)} %all-gather.4.cloned.1.call-done) | copy-start | bytes 5111812
  211.5 4.7 %copy-start.11 = (bf16[128,8192]{1,0:T(8,128)(2,1)S(1)}, bf16[128,8192]{1,0:T(8,128)(2,1)}, u32[]{:S(2)}) copy-start(bf16[128,8192]{1,0:T(8,128)(2,1)} %all-gather.6.cloned.1.call-done) | copy-start | bytes 6291460
Sparse Core Ops, SparseCore 0:
  131.8 20.6 all-gather.3
  154.6 22.5 all-gather.5
  178.8 22.5 all-gather.7

commit v2 on v1

--- a/solution.py
+++ b/solution.py
@@ -9,6 +9,7 @@
 
 MESH = pl.DeviceIdType.MESH
 bf16 = jnp.bfloat16
+vmem_grant = 60 * 2**20
 f32 = jnp.float32
 
 
@@ -49,7 +50,7 @@
 
 
 def gather_kernel(
-    blocks, x_ref, d_ref, xo_ref, do_ref, own_sem, up_s, up_r, dn_s, dn_r, ac_s, ac_r, ex_s, ex_r
+    blocks, x_ref, d_ref, xo_ref, do_ref, hold, own_sem, up_s, up_r, dn_s, dn_r, ac_s, ac_r, ex_s, ex_r
 ):
     me, line, row, col, partner = place(blocks)
     outs = (xo_ref, do_ref)
@@ -92,8 +93,14 @@
         def _():
             dn_copy(c, ins[c], me, 0).start()
 
+    loads = []
     for c in range(2):
-        copy = pltpu.make_async_copy(ins[c], outs[c].at[me], own_sem.at[c])
+        copy = pltpu.make_async_copy(ins[c], hold.at[c], own_sem.at[0, c])
+        copy.start()
+        loads.append(copy)
+    for c in range(2):
+        loads[c].wait()
+        copy = pltpu.make_async_copy(hold.at[c], outs[c].at[me], own_sem.at[1, c])
         copy.start()
         own.append(copy)
     for s in range(1, line):
@@ -187,9 +194,9 @@
         out_shape=(shape, shape),
         in_specs=[pl.BlockSpec(memory_space=pl.ANY)] * 2,
         out_specs=(pl.BlockSpec(memory_space=pl.ANY),) * 2,
-        scratch_shapes=[dma((2,))] + [dma((2, line))] * 6 + [dma((2,))] * 2,
+        scratch_shapes=[pltpu.VMEM((2,) + x.shape, x.dtype), dma((2, 2))] + [dma((2, line))] * 6 + [dma((2,))] * 2,
         compiler_params=pltpu.CompilerParams(
-            collective_id=0, has_side_effects=True, vmem_limit_bytes=4 * 2**20
+            collective_id=0, has_side_effects=True, vmem_limit_bytes=vmem_grant
         ),
         name="gather_rows",
     )(x, dy)
@@ -568,7 +575,7 @@
         ],
         out_specs=(whole(rows, units),) * 3 + (whole(3 * rank, rows),),
         scratch_shapes=[pltpu.VMEM((rows, own), f32)] * 3,
-        compiler_params=pltpu.CompilerParams(vmem_limit_bytes=32 * 2**20),
+        compiler_params=pltpu.CompilerParams(vmem_limit_bytes=vmem_grant),
         cost_estimate=pl.CostEstimate(
             flops=6 * rows * width * (units + own),
             bytes_accessed=6 * width * (units + own),
@@ -640,7 +647,7 @@
         out_specs=(whole(rows, units),) * 3 + (whole(3 * rank, rows),),
         scratch_shapes=[pltpu.VMEM((rows, units), f32)] * 3
         + [pltpu.VMEM((3 * rank, rows), f32)],
-        compiler_params=pltpu.CompilerParams(vmem_limit_bytes=32 * 2**20),
+        compiler_params=pltpu.CompilerParams(vmem_limit_bytes=vmem_grant),
         cost_estimate=pl.CostEstimate(
             flops=12 * rows * total * units,
             bytes_accessed=12 * total * units,
@@ -688,7 +695,7 @@
         + [down(units), down(units), across(units), across(own), across(own), across(own)],
         out_specs=(across(rows), across(rows)),
         scratch_shapes=[pltpu.VMEM((rows, own), bf16)] * 3,
-        compiler_params=pltpu.CompilerParams(vmem_limit_bytes=32 * 2**20),
+        compiler_params=pltpu.CompilerParams(vmem_limit_bytes=vmem_grant),
         cost_estimate=pl.CostEstimate(
             flops=6 * rows * width * (units + own),
             bytes_accessed=6 * width * (units + own),
@@ -696,6 +703,47 @@
         ),
         name="output_terms",
     )(hid, gg, gu, sums, slot, pat, gw, uw, dw, ag, au, bd)
+
+
+def grads_kernel(rank, coeffs, owner, pat, *refs):
+    count = len(refs) // 3
+    values, outs, weights = refs[:count], refs[count : 2 * count], refs[2 * count :]
+
+    @pl.when(pl.program_id(1) == 0)
+    def _():
+        entries = pat.shape[0]
+        line = lax.broadcasted_iota(jnp.int32, (entries, 1), 0) // rank
+        mask = line + pl.program_id(0) * (entries // rank) == owner[...]
+        for k, ref in enumerate(weights):
+            given = coeffs[:, k * rank : (k + 1) * rank]
+            ref[...] = jnp.where(mask, dot(pat[...], given, ((1,), (1,))), 0.0).astype(bf16)
+
+    for value, out, weight in zip(values, outs, weights):
+        out[...] = dot(weight[...], value[...])
+
+
+def outer_sums(rank, entries, coeffs, owner, values, columns, name):
+    rows, width = values[0][0].shape[0], columns
+    tall = min(256, entries * rank)
+    tile = min(1024, width)
+    pat = jnp.transpose(ranks_pattern(rank, tall // rank))
+    whole = lambda *shape: pl.BlockSpec(shape, lambda i, j: (0, 0))
+    out = jax.ShapeDtypeStruct((entries * rank, width), f32)
+    found = pl.pallas_call(
+        functools.partial(grads_kernel, rank),
+        grid=(entries * rank // tall, width // tile),
+        out_shape=(out,) * len(values),
+        in_specs=[whole(rows, coeffs.shape[1]), whole(1, rows), whole(*pat.shape)]
+        + [
+            pl.BlockSpec((rows, tile), lambda i, j, at=start // tile: (0, at + j))
+            for _, start in values
+        ],
+        out_specs=(pl.BlockSpec((tall, tile), lambda i, j: (i, j)),) * len(values),
+        scratch_shapes=[pltpu.VMEM((tall, rows), bf16)] * len(values),
+        compiler_params=pltpu.CompilerParams(vmem_limit_bytes=vmem_grant),
+        name=name,
+    )(coeffs, owner, pat, *[value for value, _ in values])
+    return [part.reshape(entries, rank, width) for part in found]
 
 
 def local(
@@ -799,34 +847,29 @@
     picked = picked.reshape(grp_count * capacity, 3 * rank)
     slots_dev = per_owner // grp_count
     first_slot = blk_index * per_owner + grp_index * slots_dev
-    slot_of_line = first_slot + jnp.arange(slots_dev * rank, dtype=jnp.int32) // rank
-    line_mask = slot_of_line[:, None] == picked_slot
-    line_pattern = ranks_pattern(rank, slots_dev)
-
-    def slot_grad(values, entries):
-        weights = dot(line_pattern, values, ((0,), (1,)))
-        weights = jnp.where(line_mask, weights, 0.0).astype(bf16)
-        return dot(weights, entries).reshape(slots_dev, rank, width)
-
-    grad_bd = slot_grad(twice * picked[:, :rank], all_dy)
-    grad_ag = slot_grad(picked[:, rank : 2 * rank], all_x)
-    grad_au = slot_grad(picked[:, 2 * rank :], all_x)
-
+    picked = jnp.concatenate((twice * picked[:, :rank], picked[:, rank:]), axis=1)
+    grad_bd, grad_ag, grad_au = outer_sums(
+        rank,
+        slots_dev,
+        picked,
+        picked_slot - first_slot,
+        ((all_dy, 0), (all_x, 0), (all_x, 0)),
+        width,
+        "slot_grads",
+    )
     tenant_dev = tenant_count // grp_count
-    tenant_of_line = grp_index * tenant_dev + jnp.arange(tenant_dev * rank, dtype=jnp.int32) // rank
-    member = tenant_of_line[:, None] == all_tenants.reshape(1, -1)
-    member_pattern = ranks_pattern(rank, tenant_dev)
-
-    def tenant_grad(values, entries):
-        weights = dot(member_pattern, values, ((0,), (1,)))
-        weights = jnp.where(member, weights, 0.0).astype(bf16)
-        return dot(weights, entries).reshape(tenant_dev, rank, units)
-
-    grad_bg = tenant_grad(twice * all_small[:, :rank], everyone[:, units : 2 * units])
-    grad_bu = tenant_grad(
-        twice * all_small[:, rank : 2 * rank], everyone[:, 2 * units : 3 * units]
-    )
-    grad_ad = tenant_grad(all_small[:, 2 * rank : 3 * rank], everyone[:, :units])
+    given = jnp.concatenate(
+        (twice * all_small[:, : 2 * rank], all_small[:, 2 * rank : 3 * rank]), axis=1
+    )
+    grad_bg, grad_bu, grad_ad = outer_sums(
+        rank,
+        tenant_dev,
+        given,
+        all_tenants.reshape(1, -1) - grp_index * tenant_dev,
+        ((everyone, units), (everyone, 2 * units), (everyone, 0)),
+        units,
+        "tenant_grads",
+    )
     return (mixed, input_grad, grad_ag, grad_au, grad_bd, grad_bg, grad_bu, grad_ad)
 
 

time: 233 us -> 233 us (level)
  Pallas kernels: 160 us -> 191 us
  matrix products: 24.6 us -> 4.28 us
  local copies, waits for them, and re-layouts: 30.1 us -> 15.5 us
  other arithmetic: 1.49 us -> 5.91 us
    unnamed x28 -> x18, local copies, waits for them, and re-layouts: 26.7 us -> 6.29 us
    dot_general x8 -> x2, matrix products: 24.4 us -> 4.13 us  [dot(): return lax.dot_general(a, b, (dims, ((), ())), preferred_element_type=f32)]
    pallas_call x0 -> x2, Pallas kernels: none -> 15.4 us  [outer_sums(): pl.pallas_call(functools.partial(grads_kernel, rank), grid=(entries * ran...]
    pallas_call x1, Pallas kernels: 11 us -> 16.2 us  [middle_terms(): pl.pallas_call(functools.partial(middle_kernel, rank), grid=(2, total //...]
    pallas_call x1, Pallas kernels: 20.7 us -> 25.5 us  [output_terms(): pl.pallas_call(functools.partial(outputs_kernel, rank), grid=(width // ti...]
    pallas_call x1, Pallas kernels: 22.4 us -> 27.2 us  [input_terms(): pl.pallas_call(functools.partial(inputs_kernel, rank), grid=(width // til...]
    convert_element_type x2 -> x4, other arithmetic: 0.02 us -> 2.75 us  [ranks_pattern(): return (column % rank == row).astype(bf16)]
  transfers between devices with their start and end apart: 3 -> 3, of which waited for: 0 -> 0; matrix products, arithmetic and copies ran while one was open for 8% -> 3% of each run, Pallas kernels for 26% -> 31%
where the time goes in v2:
time: 233 us; the launch traced here: 232 us
  Pallas kernels  191 us (82%)
  local copies, waits for them, and re-layouts  15.5 us (7%)
  between operations  14 us (6%)
  other arithmetic  5.91 us (3%)
  matrix products  4.28 us (2%)
    pallas_call x1, Pallas kernels, gather_rows(): pl.pallas_call(functools.partial(gather_kernel, blocks), out_shape=(shape...  52.5 us
    pallas_call x1, Pallas kernels, scatter_rows(): pl.pallas_call(functools.partial(scatter_kernel, blocks), out_shape=(bloc...  40.5 us
    pallas_call x1, Pallas kernels, input_terms(): pl.pallas_call(functools.partial(inputs_kernel, rank), grid=(width // til...  27.2 us
    pallas_call x1, Pallas kernels, output_terms(): pl.pallas_call(functools.partial(outputs_kernel, rank), grid=(width // ti...  25.5 us
    pallas_call x1, Pallas kernels, middle_terms(): pl.pallas_call(functools.partial(middle_kernel, rank), grid=(2, total //...  16.2 us
    pallas_call x2, Pallas kernels, outer_sums(): pl.pallas_call(functools.partial(grads_kernel, rank), grid=(entries * ran...  15.4 us
    pallas_call x2, Pallas kernels, sum_over_blk(): pl.pallas_call(functools.partial(sum_kernel, blocks), out_shape=jax.Shape...  13.2 us
    unnamed x18, local copies, waits for them, and re-layouts  6.29 us
  transfers between devices with their start and end apart: 3, of which 0 were waited for; matrix products, arithmetic and copies ran while one was open for 3% of the time, Pallas kernels for 31%

profile of v2, /device:TPU:0, one launch (start us, length us, event | category | flops | bytes accessed | tf_op | source)
XLA Modules:
  0.0 231.8 jit_solution(9064879076095082987)
XLA Ops:
  7.2 0.0 all-gather.4.cloned.1.call-start
  7.3 0.8 reshape.166
  8.0 0.1 eq.66
  8.1 0.9 select_reduce_fusion
  9.1 0.7 copy.68.slot
  9.8 0.3 reduce_window_sum.11
  10.1 52.5 %gather_rows.1 = (bf16[8,16,8192]{2,1,0:T(8,128)(2,1)}, bf16[8,16,8192]{2,1,0:T(8,128)(2,1)}) custom-call(bf16[16,8192]{1,0:T(8,128)(2,1)} %x_ref.1, bf16[16,8192]{1,0:T(8,128)(2,1)} %d_ref.1), custom_call_target="tpu_custom_call" | custom-call | tf_op jit(solution)/shard_map/gather_rows/pallas_call | solution.py:192
  62.7 2.9 %convolution_convert_fusion.1 = bf16[32,8192]{1,0:T(8,128)(2,1)} fusion(bf16[128,8192]{1,0:T(8,128)(2,1)} %bitcast.46, pred[4,32,128]{2,1,0:T(32,128)(4,1)S(1)} %fusion.1, s32[]{:T(128)S(6)} %select_n.58), kind=kOutput, calls=%fused_computation.1 | convolution fusion | flops 67371008 | bytes 2625540 | tf_op jit(solution)/shard_map/dot_general | solution.py:499
  65.7 1.2 convolution_convert_fusion
  66.9 0.6 fusion.4.pat
  67.5 27.2 %input_terms.1 = (f32[128,512]{1,0:T(8,128)}, f32[128,512]{1,0:T(8,128)}, f32[128,512]{1,0:T(8,128)}, bf16[48,128]{1,0:T(8,128)(2,1)}) custom-call(bf16[128,8192]{1,0:T(8,128)(2,1)} %bitcast.47, bf16[128,8192]{1,0:T(8,128)(2,1)} %bitcast.48, bf16[8192,512]{1,0:T(8,128)(2,1)} %gw.3, bf16[8192,512]{1,0:T(8,128)(2,1)} %uw.3, bf16[512,8192]{1,0:T(8,128)(2,1)} %dw.3, ...), custom_call_target="tpu_custom_call" | custom-call | flops 6442450944 | bytes 50331648 | tf_op jit(solution)/shard_map/input_terms/pallas_call | solution.py:560
  94.7 0.7 copy-done.3
  95.4 6.6 %sum_over_blk.2 = bf16[48,128]{1,0:T(8,128)(2,1)S(1)} custom-call(bf16[48,128]{1,0:T(8,128)(2,1)S(1)} %copy-done.3), custom_call_target="tpu_custom_call" | custom-call | tf_op jit(solution)/shard_map/sum_over_blk/pallas_call | solution.py:473
  102.0 0.7 copy.69
  102.7 0.7 copy.70.tenant
  103.4 0.6 fusion.2.pat
  104.0 16.2 %middle_terms.1 = (bf16[128,512]{1,0:T(8,128)(2,1)}, bf16[128,512]{1,0:T(8,128)(2,1)}, bf16[128,512]{1,0:T(8,128)(2,1)}, bf16[48,128]{1,0:T(8,128)(2,1)}) custom-call(f32[128,512]{1,0:T(8,128)} %get-tuple-element.33.gate, f32[128,512]{1,0:T(8,128)} %get-tuple-element.34.up, f32[128,512]{1,0:T(8,128)} %get-tuple-element.35.gh, bf16[128,48]{1,0:T(8,128)(2,1)} %bitcast.56, ...), custom_call_target="tpu_custom_call" | custom-call | flops 3221225472 | bytes 25165824 | tf_op jit(solution)/shard_map/middle_terms/pallas_call | solution.py:640
  120.3 0.7 copy-done.2
  121.0 6.7 %sum_over_blk.3 = bf16[48,128]{1,0:T(8,128)(2,1)S(1)} custom-call(bf16[48,128]{1,0:T(8,128)(2,1)S(1)} %copy-done.2), custom_call_target="tpu_custom_call" | custom-call | tf_op jit(solution)/shard_map/sum_over_blk/pallas_call | solution.py:473
  127.7 0.1 copy.71
  127.8 1.1 concatenate.9
  129.0 0.8 pad.4
  129.8 0.0 all-gather.6.cloned.1.call-start
  129.8 0.7 all-gather.6.cloned.1.call-update
  130.5 0.0 all-gather.8.cloned.1.call-start
  130.6 0.7 all-gather.8.cloned.1.call-update
  131.3 25.5 %output_terms.1 = (bf16[128,8192]{1,0:T(8,128)(2,1)}, bf16[128,8192]{1,0:T(8,128)(2,1)}) custom-call(bf16[128,512]{1,0:T(8,128)(2,1)} %get-tuple-element.38.hid, bf16[128,512]{1,0:T(8,128)(2,1)} %get-tuple-element.39.gg, bf16[128,512]{1,0:T(8,128)(2,1)} %get-tuple-element.40.gu, bf16[128,48]{1,0:T(8,128)(2,1)} %bitcast.55, s32[128,1]{1,0:T(8,128)} %copy.68.slot, ...), custom_call_target="tpu_custom_call" | custom-call | flops 6442450944 | bytes 50331648 | tf_op jit(solution)/shard_map/output_terms/pallas_call | solution.py:689
  156.8 1.6 copy-done
  158.4 1.7 copy-done.1
  160.1 40.5 %scatter_rows.1 = (bf16[16,8192]{1,0:T(8,128)(2,1)S(1)}, bf16[16,8192]{1,0:T(8,128)(2,1)S(1)}) custom-call(bf16[8,16,8192]{2,1,0:T(8,128)(2,1)S(1)} %bitcast.38, bf16[8,16,8192]{2,1,0:T(8,128)(2,1)S(1)} %bitcast.39), custom_call_target="tpu_custom_call" | custom-call | tf_op jit(solution)/shard_map/scatter_rows/pallas_call | solution.py:421
  200.6 0.1 select_reduce_fusion.1
  200.8 0.6 sub.49.owner
  201.4 0.7 sub.52.owner
  202.1 0.7 fusion.3.pat
  202.8 0.8 fusion.pat
  203.6 1.0 slice.24
  204.7 0.1 convolution_convert_fusion.2
  204.8 0.1 slice.26
  204.9 0.1 copy.79
  205.0 0.1 copy.78
  205.1 0.8 copy.76.coeffs
  205.8 1.0 slice.28
  206.8 0.9 slice_multiply_fusion
  207.7 0.8 pad_maximum_fusion.coeffs
  208.5 5.5 %tenant_grads.1 = (f32[1024,512]{1,0:T(8,128)}, f32[1024,512]{1,0:T(8,128)}, f32[1024,512]{1,0:T(8,128)}) custom-call(bf16[512,48]{1,0:T(8,128)(2,1)} %pad_maximum_fusion.coeffs, s32[1,512]{1,0:T(1,128)} %sub.52.owner, bf16[256,16]{1,0:T(8,128)(2,1)} %fusion.pat, bf16[512,1664]{1,0:T(8,128)(2,1)} %all-gather.4.cloned.1.call-done.refs_0_.refs_1_.refs_2_, ...), custom_call_target="tpu_custom_call" | custom-call | tf_op jit(solution)/shard_map/tenant_grads/pallas_call | solution.py:732
  214.0 9.8 %slot_grads.1 = (f32[128,8192]{1,0:T(8,128)}, f32[128,8192]{1,0:T(8,128)}, f32[128,8192]{1,0:T(8,128)}) custom-call(bf16[128,48]{1,0:T(8,128)(2,1)} %copy.76.coeffs, s32[1,128]{1,0:T(1,128)} %sub.49.owner, bf16[128,16]{1,0:T(8,128)(2,1)} %fusion.3.pat, bf16[128,8192]{1,0:T(8,128)(2,1)} %all-gather.6.cloned.1.call-done.refs_0_, ...), custom_call_target="tpu_custom_call" | custom-call | tf_op jit(solution)/shard_map/slot_grads/pallas_call | solution.py:732
  223.9 0.7 copy.89
  224.6 0.7 copy.90
  (31 shorter events, 0.2 us)
Async XLA Ops:
  7.2 196.5 %all-gather.4.cloned.1.call-start = ((), (), s32[]{:S(2)}) async-start(), calls=%async_computation | async-start | bytes 2129920 | tf_op jit(solution)/shard_map/all_gather | solution.py:821
  62.7 3.0 %copy-start.4 = (bf16[8,16,8192]{2,1,0:T(8,128)(2,1)S(1)}, bf16[8,16,8192]{2,1,0:T(8,128)(2,1)}, u32[]{:S(2)}) copy-start(bf16[8,16,8192]{2,1,0:T(8,128)(2,1)} %get-tuple-element.32) | copy-start | bytes 6291460
  94.7 0.7 copy-start.3
  104.0 23.8 %copy-start.6 = (bf16[48,128]{0,1:T(8,128)(2,1)S(1)}, bf16[48,128]{0,1:T(8,128)(2,1)}, u32[]{:S(2)}) copy-start(bf16[48,128]{0,1:T(8,128)(2,1)} %copy.69) | copy-start | bytes 36868
  120.3 0.7 copy-start.2
  127.8 3.5 %copy-start.5 = (bf16[48,128]{0,1:T(8,128)(2,1)}, bf16[48,128]{0,1:T(8,128)(2,1)S(1)}, u32[]{:S(2)}) copy-start(bf16[48,128]{0,1:T(8,128)(2,1)S(1)} %copy.71) | copy-start | bytes 36868
  129.8 84.3 %all-gather.6.cloned.1.call-start = ((), (), s32[]{:S(2)}) async-start(), calls=%async_computation.1 | async-start | bytes 2621440 | tf_op jit(solution)/shard_map/all_gather | solution.py:810
  130.5 83.5 %all-gather.8.cloned.1.call-start = ((), (), s32[]{:S(2)}) async-start(), calls=%async_computation.2 | async-start | bytes 2621440 | tf_op jit(solution)/shard_map/all_gather | solution.py:809
  156.8 1.6 copy-start
  158.4 1.7 copy-start.1
Sparse Core Ops, SparseCore 0:
  129.9 20.6 all-gather.3
  152.7 22.5 all-gather.5
  177.5 22.5 all-gather.7
